TPU v7x, 1024 devices: a whole 4x8x16 slice. The times are simulated.
1024 devices in a mesh: tm: 64 (over x_hi, z, core), space: 16 (over x_lo, y).
Axes of the slice: x: 4 (x_hi: 2, x_lo: 2; x = x_hi * 2 + x_lo), y: 8, z: 16, core: 2. Of those that a mesh axis runs over, the one named last changes fastest.
Arguments:
- y_first: bfloat16 [2, 64, 1024, 1024], P(None, 'tm', 'space'), may hold values from -6 to 6
- y_second: bfloat16 [2, 64, 1024, 1024], P(None, 'tm', 'space'), may hold values from -6 to 6
- grad_first: bfloat16 [2, 64, 1024, 1024], P(None, 'tm', 'space'), may hold values from -6 to 6
- grad_second: bfloat16 [2, 64, 1024, 1024], P(None, 'tm', 'space'), may hold values from -6 to 6
- pattern: int32 [64, 8], P('tm'), may hold values from 0 to 7, as said below
- time_qkv: bfloat16 [1024, 1536], replicated, may hold values from -3 to 3
- time_out: bfloat16 [512, 1024], replicated, may hold values from -0.25 to 0.25
- space_qkv: bfloat16 [1024, 1536], replicated, may hold values from -3 to 3
- space_out: bfloat16 [512, 1024], replicated, may hold values from -0.25 to 0.25
Outputs:
- x_first: bfloat16 [2, 64, 1024, 1024], P(None, 'tm', 'space')
- x_second: bfloat16 [2, 64, 1024, 1024], P(None, 'tm', 'space')
- dx_first: bfloat16 [2, 64, 1024, 1024], P(None, 'tm', 'space')
- dx_second: bfloat16 [2, 64, 1024, 1024], P(None, 'tm', 'space')
Inputs may be any that keep to these rules, and one draw needn't show every extreme that they name: pattern[f, b] is b - 1, b or b + 1.
All inputs are finite; a program needn't handle non-finite values.
Results may differ from a plain program's by a relative error of at most 0.01.
Values may be sent and summed in bfloat16 or wider, within the bound.
No kernel may reach another device: no remote copies, remote signals or barrier semaphores. Data moves between devices by JAX's collectives and lax.ppermute only.
A program may use at most 64 MiB of HBM per device.

v0:
```python
import jax
import jax.numpy as jnp
from jax import lax
from jax.sharding import PartitionSpec as P

HEADS = 8
HEAD_DIM = 64


EPSILON = 1e-05


def from_behind(block, axis, distance):
    devices = range(lax.axis_size(axis))
    route = [(i - distance, i) for i in devices if i - distance in devices]
    return lax.ppermute(block, axis, route)


def normed(rows):
    values_f = rows.astype(jnp.float32)
    center = values_f - jnp.mean(values_f, -1, keepdims=True)
    inv_std = lax.rsqrt(jnp.mean(center * center, -1, keepdims=True) + EPSILON)
    return (center * inv_std, inv_std)


def norm_back(rows, grad_in):
    normal_rows, inv_std = normed(rows)
    return inv_std * (
        grad_in
        - jnp.mean(grad_in, -1, keepdims=True)
        - normal_rows * jnp.mean(grad_in * normal_rows, -1, keepdims=True)
    )


def matmul_f32(left, right):
    return jnp.dot(left, right, preferred_element_type=jnp.float32)


def matmul_tr(left, right):
    return lax.dot_general(
        left, right, (((left.ndim - 1,), (1,)), ((), ())), preferred_element_type=jnp.float32
    )


def contract(spec, left, right):
    return jnp.einsum(spec, left, right, preferred_element_type=jnp.float32)


def attend(queries, key_rows, value_rows, query_spec, key_spec, score_spec):
    factor = queries.shape[-1] ** (-0.5)
    scores = contract(query_spec + "," + key_spec + "->" + score_spec, queries, key_rows) * factor
    weights = jax.nn.softmax(scores, axis=-1)
    mixed_rows = contract(
        score_spec + "," + key_spec + "->" + query_spec, weights.astype(jnp.bfloat16), value_rows
    )
    return (mixed_rows.astype(jnp.bfloat16), weights)


def attend_back(queries, key_rows, value_rows, weights, out_grad, query_spec, key_spec, score_spec):
    factor = queries.shape[-1] ** (-0.5)
    value_grad = contract(
        score_spec + "," + query_spec + "->" + key_spec, weights.astype(jnp.bfloat16), out_grad
    )
    weight_grad = contract(query_spec + "," + key_spec + "->" + score_spec, out_grad, value_rows)
    row_delta = jnp.sum(weights * weight_grad, -1, keepdims=True)
    score_grad = (weights * (weight_grad - row_delta)).astype(jnp.bfloat16)
    query_grad = (
        contract(score_spec + "," + key_spec + "->" + query_spec, score_grad, key_rows) * factor
    )
    key_grad = (
        contract(score_spec + "," + query_spec + "->" + key_spec, score_grad, queries) * factor
    )
    return (query_grad, key_grad, value_grad)


def to_frames(rows):
    flipped = jnp.swapaxes(rows, 1, 2)
    return lax.all_to_all(flipped, "tm", split_axis=1, concat_axis=2, tiled=True)


def to_patches(rows):
    back = lax.all_to_all(rows, "tm", split_axis=2, concat_axis=1, tiled=True)
    return jnp.swapaxes(back, 1, 2)


def per_device(
    y_first, y_second, grad_first, grad_second, pattern, time_qkv, time_out, space_qkv, space_out
):
    clips, frames_dev, patches_dev, unused_w = y_first.shape
    inner_w = time_out.shape[0]
    position = lax.axis_index("space")
    block_id = position // 2
    neighbour = lax.dynamic_index_in_dim(pattern, block_id, 1, keepdims=False)
    own_block = jnp.broadcast_to(block_id, neighbour.shape)
    shard_ids = jnp.stack([2 * own_block, 2 * own_block + 1, 2 * neighbour, 2 * neighbour + 1], 1)
    slot_ids = shard_ids - position + 3
    selector = (slot_ids[:, :, None] == jnp.arange(7, dtype=jnp.int32)[None, None, :]).astype(
        jnp.bfloat16
    )
    normal_first, unused = normed(y_first)
    space_proj = matmul_f32(normal_first.astype(jnp.bfloat16), space_qkv).astype(jnp.bfloat16)
    space_queries = space_proj[..., :inner_w].reshape(
        clips, frames_dev, patches_dev, HEADS, HEAD_DIM
    )
    key_value = space_proj[..., inner_w:]
    pieces = []
    for offset in range(-3, 4):
        if offset == 0:
            pieces.append(key_value)
        else:
            pieces.append(from_behind(key_value, "space", -offset))
    window = contract("fjo,ocfpx->cfjpx", selector, jnp.stack(pieces, 0)).astype(jnp.bfloat16)
    window = window.reshape(clips, frames_dev, 4 * patches_dev, 2, HEADS, HEAD_DIM)
    space_keys = window[:, :, :, 0]
    space_values = window[:, :, :, 1]
    space_mixed, space_weights = attend(
        space_queries, space_keys, space_values, "cfqhe", "cfkhe", "cfhqk"
    )
    space_value = matmul_f32(
        space_mixed.reshape(clips, frames_dev, patches_dev, inner_w), space_out
    )
    x_second = (y_second.astype(jnp.float32) - space_value).astype(jnp.bfloat16)
    normal_second, unused = normed(x_second)
    time_proj = matmul_f32(normal_second.astype(jnp.bfloat16), time_qkv).astype(jnp.bfloat16)
    time_rows = to_frames(time_proj)
    per_patch = time_rows.shape[1]
    all_frames = time_rows.shape[2]
    split_rows = time_rows.reshape(clips, per_patch, all_frames, 3, HEADS, HEAD_DIM)
    time_mixed, time_weights = attend(
        split_rows[:, :, :, 0],
        split_rows[:, :, :, 1],
        split_rows[:, :, :, 2],
        "cpfhe",
        "cpghe",
        "cphfg",
    )
    time_back = to_patches(time_mixed.reshape(clips, per_patch, all_frames, inner_w))
    x_first = (y_first.astype(jnp.float32) - matmul_f32(time_back, time_out)).astype(jnp.bfloat16)
    space_grad = matmul_tr(grad_second, space_out).astype(jnp.bfloat16)
    space_grad = space_grad.reshape(clips, frames_dev, patches_dev, HEADS, HEAD_DIM)
    query_grad, key_grad, value_grad = attend_back(
        space_queries,
        space_keys,
        space_values,
        space_weights,
        space_grad,
        "cfqhe",
        "cfkhe",
        "cfhqk",
    )
    slot_shape = (clips, frames_dev, 4, patches_dev, inner_w)
    window_grad = jnp.concatenate(
        [
            key_grad.astype(jnp.bfloat16).reshape(slot_shape),
            value_grad.astype(jnp.bfloat16).reshape(slot_shape),
        ],
        -1,
    )
    spread = contract("fjo,cfjpx->ocfpx", selector, window_grad).astype(jnp.bfloat16)
    gathered = spread[3].astype(jnp.float32)
    for offset in range(-3, 4):
        if offset != 0:
            gathered = gathered + from_behind(spread[offset + 3], "space", offset).astype(
                jnp.float32
            )
    space_dqkv = jnp.concatenate(
        [
            query_grad.astype(jnp.bfloat16).reshape(clips, frames_dev, patches_dev, inner_w),
            gathered.astype(jnp.bfloat16),
        ],
        -1,
    )
    dx_first = (
        grad_first.astype(jnp.float32) + norm_back(y_first, matmul_tr(space_dqkv, space_qkv))
    ).astype(jnp.bfloat16)
    time_grad = matmul_tr(dx_first, time_out).astype(jnp.bfloat16)
    time_grad_rows = to_frames(time_grad).reshape(clips, per_patch, all_frames, HEADS, HEAD_DIM)
    time_grads = attend_back(
        split_rows[:, :, :, 0],
        split_rows[:, :, :, 1],
        split_rows[:, :, :, 2],
        time_weights,
        time_grad_rows,
        "cpfhe",
        "cpghe",
        "cphfg",
    )
    time_dqkv = (
        jnp.stack(time_grads, 3)
        .astype(jnp.bfloat16)
        .reshape(clips, per_patch, all_frames, 3 * inner_w)
    )
    dqkv_back = to_patches(time_dqkv)
    dx_second = (
        grad_second.astype(jnp.float32) + norm_back(x_second, matmul_tr(dqkv_back, time_qkv))
    ).astype(jnp.bfloat16)
    return (x_first, x_second, dx_first, dx_second)


def solution(mesh):
    in_specs = (
        P(None, "tm", "space", None),
        P(None, "tm", "space", None),
        P(None, "tm", "space", None),
        P(None, "tm", "space", None),
        P("tm", None),
        P(),
        P(),
        P(),
        P(),
    )
    out_specs = (
        P(None, "tm", "space", None),
        P(None, "tm", "space", None),
        P(None, "tm", "space", None),
        P(None, "tm", "space", None),
    )
    return jax.shard_map(
        per_device, mesh=mesh, in_specs=in_specs, out_specs=out_specs, check_vma=False
    )
```

profile of v0, /device:TPU:25, one launch (start us, length us, event | category | flops | bytes accessed | tf_op | source)
XLA Modules:
  0.0 345.9 jit_solution(5542994652108066132)
XLA Ops:
  5.4 4.6 %collective-permute-start = (bf16[2,1,64,1024]{3,2,0,1:T(8,128)(2,1)}, bf16[2,1,64,1024]{3,2,0,1:T(8,128)(2,1)}, u32[]{:S(2)}, u32[]{:S(2)}) collective-permute-start(bf16[2,1,64,1024]{3,2,0,1:T(8,128)(2,1)} %slice.59), channel_id=1, source_target_pairs={{0,3},{1,4},{2,5},{3,6},{4,7},{5,8},{6,9},{7,10},{8,11},{9,12},{10... | collective-permute-start | bytes 786440 | tf_op jit(solution)/shard_map/ppermute | solution.py:16
  10.1 2.4 collective-permute-start.1
  12.5 3.2 collective-permute-start.2
  15.7 2.1 collective-permute-start.3
  17.8 5.1 %collective-permute-start.4 = (bf16[2,1,64,1024]{3,2,0,1:T(8,128)(2,1)}, bf16[2,1,64,1024]{3,2,0,1:T(8,128)(2,1)}, u32[]{:S(2)}, u32[]{:S(2)}) collective-permute-start(bf16[2,1,64,1024]{3,2,0,1:T(8,128)(2,1)} %slice.59), channel_id=1, source_target_pairs={{2,0},{3,1},{4,2},{5,3},{6,4},{7,5},{8,6},{9,7},{10,8},{11,9},{12,... | collective-permute-start | bytes 786440 | tf_op jit(solution)/shard_map/ppermute | solution.py:16
  24.2 2.5 convolution_convert_fusion.5
  34.4 4.0 %collective-permute-done.1 = bf16[2,1,64,1024]{3,2,0,1:T(8,128)(2,1)} collective-permute-done((bf16[2,1,64,1024]{3,2,0,1:T(8,128)(2,1)}, bf16[2,1,64,1024]{3,2,0,1:T(8,128)(2,1)}, u32[]{:S(2)}, u32[]{:S(2)}) %collective-permute-start.1) | collective-permute-done | bytes 262176 | tf_op jit(solution)/shard_map/ppermute | solution.py:16
  39.4 6.4 %collective-permute-done.2 = bf16[2,1,64,1024]{3,2,0,1:T(8,128)(2,1)} collective-permute-done((bf16[2,1,64,1024]{3,2,0,1:T(8,128)(2,1)}, bf16[2,1,64,1024]{3,2,0,1:T(8,128)(2,1)}, u32[]{:S(2)}, u32[]{:S(2)}) %collective-permute-start.2) | collective-permute-done | bytes 262176 | tf_op jit(solution)/shard_map/ppermute | solution.py:16
  53.2 4.0 %reshape.487 = bf16[2,1,256,2,8,64]{5,4,3,2,0,1:T(8,128)(2,1)} reshape(bf16[2,1,4,64,1024]{4,3,2,0,1:T(8,128)(2,1)} %copy.365) | data formatting | bytes 2097152 | tf_op jit(solution)/shard_map/reshape | solution.py:113
  57.2 3.0 fusion.127
  60.2 2.5 copy.436
  62.7 2.5 copy.437
  65.2 2.5 fusion.130
  67.8 2.6 fusion.36
  74.3 2.8 reshape.516
  77.0 2.6 copy.386
  79.6 2.8 reshape.517
  82.4 2.6 copy.387
  84.9 2.1 convert_bitcast_fusion
  87.1 3.5 %slice_bitcast_fusion.5 = (bf16[2,1,64,1024]{3,1,2,0:T(2,128)(2,1)}, bf16[2,1,64,1024]{3,1,2,0:T(2,128)(2,1)}, bf16[2,1,64,1024]{3,1,2,0:T(2,128)(2,1)S(1)}, bf1...) fusion(bf16[7,2,1,64,1024]{4,0,3,1,2:T(8,128)(2,1)S(1)} %convert_bitcast_fusion), kind=kLoop, calls=%fused_computation.95 | loop fusion | bytes 3145728 | tf_op jit(solution)/shard_map/squeeze | solution.py:163
  90.6 8.0 %collective-permute-start.10 = (bf16[2,1,64,1024]{3,1,2,0:T(2,128)(2,1)S(1)}, bf16[2,1,64,1024]{3,1,2,0:T(2,128)(2,1)S(1)}, u32[]{:S(2)}, u32[]{:S(2)}) collective-permute-start(bf16[2,1,64,1024]{3,1,2,0:T(2,128)(2,1)S(1)} %get-tuple-element.42), channel_id=1, source_target_pairs={{0,2},{1,3},{2,4},{3,5},{4,6},{5,7},{6,8},{7,9},{8,10},{9,11},{10,... | collective-permute-start | bytes 786440 | tf_op jit(solution)/shard_map/ppermute | solution.py:16
  98.6 4.4 %collective-permute-start.11 = (bf16[2,1,64,1024]{3,1,2,0:T(2,128)(2,1)}, bf16[2,1,64,1024]{3,1,2,0:T(2,128)(2,1)}, u32[]{:S(2)}, u32[]{:S(2)}) collective-permute-start(bf16[2,1,64,1024]{3,1,2,0:T(2,128)(2,1)} %get-tuple-element.41), channel_id=1, source_target_pairs={{0,3},{1,4},{2,5},{3,6},{4,7},{5,8},{6,9},{7,10},{8,11},{9,12},{10... | collective-permute-start | bytes 786440 | tf_op jit(solution)/shard_map/ppermute | solution.py:16
  103.0 3.5 %collective-permute-start.6 = (bf16[2,1,64,1024]{3,1,2,0:T(2,128)(2,1)}, bf16[2,1,64,1024]{3,1,2,0:T(2,128)(2,1)}, u32[]{:S(2)}, u32[]{:S(2)}) collective-permute-start(bf16[2,1,64,1024]{3,1,2,0:T(2,128)(2,1)} %get-tuple-element.40), channel_id=1, source_target_pairs={{3,0},{4,1},{5,2},{6,3},{7,4},{8,5},{9,6},{10,7},{11,8},{12,9},{13... | collective-permute-start | bytes 786440 | tf_op jit(solution)/shard_map/ppermute | solution.py:16
  106.5 2.9 collective-permute-start.7
  109.4 1.9 collective-permute-start.8
  113.2 13.2 %collective-permute-start.9 = (bf16[2,1,64,1024]{3,1,2,0:T(2,128)(2,1)}, bf16[2,1,64,1024]{3,1,2,0:T(2,128)(2,1)}, u32[]{:S(2)}, u32[]{:S(2)}) collective-permute-start(bf16[2,1,64,1024]{3,1,2,0:T(2,128)(2,1)} %get-tuple-element.43), channel_id=1, source_target_pairs={{0,1},{1,2},{2,3},{3,4},{4,5},{5,6},{6,7},{7,8},{8,9},{9,10},{10,1... | collective-permute-start | bytes 786440 | tf_op jit(solution)/shard_map/ppermute | solution.py:16
  127.7 28.6 %collective-permute-done.11 = bf16[2,1,64,1024]{3,1,2,0:T(2,128)(2,1)} collective-permute-done((bf16[2,1,64,1024]{3,1,2,0:T(2,128)(2,1)}, bf16[2,1,64,1024]{3,1,2,0:T(2,128)(2,1)}, u32[]{:S(2)}, u32[]{:S(2)}) %collective-permute-start.11) | collective-permute-done | bytes 262176 | tf_op jit(solution)/shard_map/ppermute | solution.py:16
  156.3 7.8 %collective-permute-done.7 = bf16[2,1,64,1024]{3,1,2,0:T(2,128)(2,1)} collective-permute-done((bf16[2,1,64,1024]{3,1,2,0:T(2,128)(2,1)}, bf16[2,1,64,1024]{3,1,2,0:T(2,128)(2,1)}, u32[]{:S(2)}, u32[]{:S(2)}) %collective-permute-start.7) | collective-permute-done | bytes 262176 | tf_op jit(solution)/shard_map/ppermute | solution.py:16
  164.1 12.3 %collective-permute-done.8 = bf16[2,1,64,1024]{3,1,2,0:T(2,128)(2,1)} collective-permute-done((bf16[2,1,64,1024]{3,1,2,0:T(2,128)(2,1)}, bf16[2,1,64,1024]{3,1,2,0:T(2,128)(2,1)}, u32[]{:S(2)}, u32[]{:S(2)}) %collective-permute-start.8) | collective-permute-done | bytes 262176 | tf_op jit(solution)/shard_map/ppermute | solution.py:16
  176.4 4.7 %add_convert_fusion = bf16[2,1,64,1024]{3,1,2,0:T(2,128)(2,1)S(1)} fusion(bf16[2,1,64,1024]{3,1,2,0:T(2,128)(2,1)} %collective-permute-done.11, bf16[2,1,64,1024]{3,1,2,0:T(2,128)(2,1)} %copy-done.16, bf16[2,1,64,1024]{3,1,2,0:T(2,128)(2,1)} %collective-permute-done.9, bf16[2,1,64,1024]{3,1,2,0:T(2,128)(2,1)} %collective-permute-done.8, ...), kind=kLoop, calls=%fused_computation.108 | loop fusion | flops 1835008 | bytes 2097152 | tf_op jit(solution)/shard_map/convert_element_type | solution.py:169
  181.9 1.9 fusion.66
  189.6 23.5 %all-to-all-start.2 = ((bf16[2,64,1,512]{3,0,2,1:T(2,128)(2,1)}), bf16[2,64,1,512]{3,0,2,1:T(2,128)(2,1)S(1)}, u32[]{:S(2)}, u32[]{:S(2)}) async-start(bf16[2,64,1,512]{3,0,2,1:T(2,128)(2,1)} %copy.396), calls=%async_computation.2 | async-start | bytes 262144 | tf_op jit(solution)/shard_map/all_to_all | solution.py:78
  214.3 2.6 fusion.16
  218.1 13.6 %all-to-all-done.2 = bf16[2,64,1,512]{3,0,2,1:T(2,128)(2,1)S(1)} async-done(((bf16[2,64,1,512]{3,0,2,1:T(2,128)(2,1)}), bf16[2,64,1,512]{3,0,2,1:T(2,128)(2,1)S(1)}, u32[]{:S(2)}, u32[]{:S(2)}) %all-to-all-start.2) | async-done | bytes 131104 | tf_op jit(solution)/shard_map/all_to_all | solution.py:78
  231.7 5.2 %all-to-all-start = ((bf16[2,64,1,1536]{3,0,2,1:T(2,128)(2,1)}), bf16[2,64,1,1536]{3,0,2,1:T(2,128)(2,1)}, u32[]{:S(2)}, u32[]{:S(2)}) async-start(bf16[2,64,1,1536]{3,0,2,1:T(2,128)(2,1)} %copy.370), calls=%async_computation | async-start | bytes 786432 | tf_op jit(solution)/shard_map/all_to_all | solution.py:78
  237.8 28.0 %all-to-all-done = bf16[2,64,1,1536]{3,0,2,1:T(2,128)(2,1)} async-done(((bf16[2,64,1,1536]{3,0,2,1:T(2,128)(2,1)}), bf16[2,64,1,1536]{3,0,2,1:T(2,128)(2,1)}, u32[]{:S(2)}, u32[]{:S(2)}) %all-to-all-start) | async-done | bytes 393248 | tf_op jit(solution)/shard_map/all_to_all | solution.py:78
  267.6 2.3 reshape.493
  269.9 2.0 fusion.128
  273.8 2.1 fusion.133
  275.9 2.1 convolution_convert_fusion.2
  281.5 4.6 %all-to-all-start.1 = ((bf16[2,1,64,512]{3,0,1,2:T(2,128)(2,1)}), bf16[2,1,64,512]{3,0,1,2:T(2,128)(2,1)S(1)}, u32[]{:S(2)}, u32[]{:S(2)}) async-start(bf16[2,1,64,512]{3,0,1,2:T(2,128)(2,1)} %copy.376), calls=%async_computation.1 | async-start | bytes 262144 | tf_op jit(solution)/shard_map/all_to_all | solution.py:82
  290.8 2.7 reshape.518
  293.5 11.1 %all-to-all-done.1 = bf16[2,1,64,512]{3,0,1,2:T(2,128)(2,1)S(1)} async-done(((bf16[2,1,64,512]{3,0,1,2:T(2,128)(2,1)}), bf16[2,1,64,512]{3,0,1,2:T(2,128)(2,1)S(1)}, u32[]{:S(2)}, u32[]{:S(2)}) %all-to-all-start.1) | async-done | bytes 131104 | tf_op jit(solution)/shard_map/all_to_all | solution.py:82
  304.6 5.2 %all-to-all-start.3 = ((bf16[2,1,64,1536]{3,0,1,2:T(2,128)(2,1)}), bf16[2,1,64,1536]{3,0,1,2:T(2,128)(2,1)}, u32[]{:S(2)}, u32[]{:S(2)}) async-start(bf16[2,1,64,1536]{3,0,1,2:T(2,128)(2,1)} %reshape.518), calls=%async_computation.3 | async-start | bytes 786432 | tf_op jit(solution)/shard_map/all_to_all | solution.py:82
  309.9 2.2 fusion.48
  312.1 26.6 %all-to-all-done.3 = bf16[2,1,64,1536]{3,0,1,2:T(2,128)(2,1)} async-done(((bf16[2,1,64,1536]{3,0,1,2:T(2,128)(2,1)}), bf16[2,1,64,1536]{3,0,1,2:T(2,128)(2,1)}, u32[]{:S(2)}, u32[]{:S(2)}) %all-to-all-start.3) | async-done | bytes 393248 | tf_op jit(solution)/shard_map/all_to_all | solution.py:82
  338.7 4.0 %fusion.72 = (f32[2,64]{1,0:T(2,128)S(1)}, f32[2,64,1024]{2,1,0:T(8,128)}) fusion(bf16[2,1,64,1024]{3,2,0,1:T(8,128)(2,1)} %get-tuple-element.54, f32[2,64]{1,0:T(2,128)S(1)} %add_rsqrt_fusion, f32[2,64]{1,0:T(2,128)S(1)} %broadcast_multiply_fusion.4, bf16[1024,1536]{1,0:T(8,128)(2,1)} %param.14, bf16[2,1,64,1536]{3,0,1,2:T(2,128)(2,1)} %all-to-all-done.3), kind=kOutput, calls=%fused_computation.84 | convolution fusion | flops 403308416 | bytes 4326912 | tf_op jit(solution)/shard_map/dot_general | solution.py:40
  343.9 2.1 fusion.91
  (108 shorter events, 51.1 us)
Async XLA Ops:
  0.6 2.4 copy-start
  3.1 19.9 %copy-start.23 = (s32[1,8]{1,0:T(1,128)S(1)}, s32[1,8]{1,0:T(1,128)}, u32[]{:S(2)}) copy-start(s32[1,8]{1,0:T(1,128)} %param.13) | copy-start | bytes 100
  5.4 26.1 %collective-permute-start = (bf16[2,1,64,1024]{3,2,0,1:T(8,128)(2,1)}, bf16[2,1,64,1024]{3,2,0,1:T(8,128)(2,1)}, u32[]{:S(2)}, u32[]{:S(2)}) collective-permute-start(bf16[2,1,64,1024]{3,2,0,1:T(8,128)(2,1)} %slice.59), channel_id=1, source_target_pairs={{0,3},{1,4},{2,5},{3,6},{4,7},{5,8},{6,9},{7,10},{8,11},{9,12},{10... | collective-permute-start | bytes 786440 | tf_op jit(solution)/shard_map/ppermute | solution.py:16
  10.1 28.4 %collective-permute-start.1 = (bf16[2,1,64,1024]{3,2,0,1:T(8,128)(2,1)}, bf16[2,1,64,1024]{3,2,0,1:T(8,128)(2,1)}, u32[]{:S(2)}, u32[]{:S(2)}) collective-permute-start(bf16[2,1,64,1024]{3,2,0,1:T(8,128)(2,1)} %slice.59), channel_id=1, source_target_pairs={{0,2},{1,3},{2,4},{3,5},{4,6},{5,7},{6,8},{7,9},{8,10},{9,11},{10,... | collective-permute-start | bytes 786440 | tf_op jit(solution)/shard_map/ppermute | solution.py:16
  12.5 33.3 %collective-permute-start.2 = (bf16[2,1,64,1024]{3,2,0,1:T(8,128)(2,1)}, bf16[2,1,64,1024]{3,2,0,1:T(8,128)(2,1)}, u32[]{:S(2)}, u32[]{:S(2)}) collective-permute-start(bf16[2,1,64,1024]{3,2,0,1:T(8,128)(2,1)} %slice.59), channel_id=1, source_target_pairs={{0,1},{1,2},{2,3},{3,4},{4,5},{5,6},{6,7},{7,8},{8,9},{9,10},{10,1... | collective-permute-start | bytes 786440 | tf_op jit(solution)/shard_map/ppermute | solution.py:16
  15.7 31.1 %collective-permute-start.3 = (bf16[2,1,64,1024]{3,2,0,1:T(8,128)(2,1)}, bf16[2,1,64,1024]{3,2,0,1:T(8,128)(2,1)}, u32[]{:S(2)}, u32[]{:S(2)}) collective-permute-start(bf16[2,1,64,1024]{3,2,0,1:T(8,128)(2,1)} %slice.59), channel_id=1, source_target_pairs={{1,0},{2,1},{3,2},{4,3},{5,4},{6,5},{7,6},{8,7},{9,8},{10,9},{11,1... | collective-permute-start | bytes 786440 | tf_op jit(solution)/shard_map/ppermute | solution.py:16
  17.8 30.0 %collective-permute-start.4 = (bf16[2,1,64,1024]{3,2,0,1:T(8,128)(2,1)}, bf16[2,1,64,1024]{3,2,0,1:T(8,128)(2,1)}, u32[]{:S(2)}, u32[]{:S(2)}) collective-permute-start(bf16[2,1,64,1024]{3,2,0,1:T(8,128)(2,1)} %slice.59), channel_id=1, source_target_pairs={{2,0},{3,1},{4,2},{5,3},{6,4},{7,5},{8,6},{9,7},{10,8},{11,9},{12,... | collective-permute-start | bytes 786440 | tf_op jit(solution)/shard_map/ppermute | solution.py:16
  31.5 19.0 %collective-permute-start.5 = (bf16[2,1,64,1024]{3,2,0,1:T(8,128)(2,1)}, bf16[2,1,64,1024]{3,2,0,1:T(8,128)(2,1)S(1)}, u32[]{:S(2)}, u32[]{:S(2)}) collective-permute-start(bf16[2,1,64,1024]{3,2,0,1:T(8,128)(2,1)} %slice.59), channel_id=1, source_target_pairs={{3,0},{4,1},{5,2},{6,3},{7,4},{8,5},{9,6},{10,7},{11,8},{12,9},{13... | collective-permute-start | bytes 786440 | tf_op jit(solution)/shard_map/ppermute | solution.py:16
  60.2 5.1 %copy-start.9 = (bf16[2,1,64,512]{2,3,0,1:T(8,128)(2,1)S(1)}, bf16[2,1,64,512]{2,3,0,1:T(8,128)(2,1)}, u32[]{:S(2)}) copy-start(bf16[2,1,64,512]{2,3,0,1:T(8,128)(2,1)} %copy.441) | copy-start | bytes 393220
  67.8 2.7 copy-start.7
  67.8 2.7 copy-start.13
  67.8 2.7 copy-start.19
  72.4 0.8 copy-start.5
  87.0 3.6 %copy-start.1 = (bf16[7,2,1,64,1024]{4,0,3,1,2:T(8,128)(2,1)}, bf16[7,2,1,64,1024]{4,0,3,1,2:T(8,128)(2,1)S(1)}, u32[]{:S(2)}) copy-start(bf16[7,2,1,64,1024]{4,0,3,1,2:T(8,128)(2,1)S(1)} %convert_bitcast_fusion) | copy-start | bytes 5505028
  87.0 24.3 %copy-start.8 = (bf16[512,1024]{1,0:T(8,128)(2,1)S(1)}, bf16[512,1024]{1,0:T(8,128)(2,1)}, u32[]{:S(2)}) copy-start(bf16[512,1024]{1,0:T(8,128)(2,1)} %param.17) | copy-start | bytes 3145732
  87.0 24.3 %copy-start.17 = (bf16[2,1,64,1024]{3,2,1,0:T(8,128)(2,1)S(1)}, bf16[2,1,64,1024]{3,2,1,0:T(8,128)(2,1)}, u32[]{:S(2)}) copy-start(bf16[2,1,64,1024]{3,2,1,0:T(8,128)(2,1)} %param.10) | copy-start | bytes 786436
  87.1 24.3 %copy-start.18 = (bf16[2,8,64,64]{3,2,1,0:T(8,128)(2,1)S(1)}, bf16[2,8,64,64]{3,2,1,0:T(8,128)(2,1)}, u32[]{:S(2)}) copy-start(bf16[2,8,64,64]{3,2,1,0:T(8,128)(2,1)} %convolution_convert_fusion.3) | copy-start | bytes 393220
  87.1 39.3 %copy-start.4 = (bf16[2,1,256,1,8,64]{2,5,4,0,3,1:T(8,128)(2,1)S(1)}, bf16[2,1,256,1,8,64]{2,5,4,0,3,1:T(8,128)(2,1)}, u32[]{:S(2)}) copy-start(bf16[2,1,256,1,8,64]{2,5,4,0,3,1:T(8,128)(2,1)} %copy.436) | copy-start | bytes 1572868
  87.1 39.3 %copy-start.6 = (bf16[2,8,64,256]{3,2,1,0:T(8,128)(2,1)S(1)}, bf16[2,8,64,256]{3,2,1,0:T(8,128)(2,1)}, u32[]{:S(2)}) copy-start(bf16[2,8,64,256]{3,2,1,0:T(8,128)(2,1)} %copy-done.5) | copy-start | bytes 1572868
  90.6 21.8 %collective-permute-start.10 = (bf16[2,1,64,1024]{3,1,2,0:T(2,128)(2,1)S(1)}, bf16[2,1,64,1024]{3,1,2,0:T(2,128)(2,1)S(1)}, u32[]{:S(2)}, u32[]{:S(2)}) collective-permute-start(bf16[2,1,64,1024]{3,1,2,0:T(2,128)(2,1)S(1)} %get-tuple-element.42), channel_id=1, source_target_pairs={{0,2},{1,3},{2,4},{3,5},{4,6},{5,7},{6,8},{7,9},{8,10},{9,11},{10,... | collective-permute-start | bytes 786440 | tf_op jit(solution)/shard_map/ppermute | solution.py:16
  98.6 57.7 %collective-permute-start.11 = (bf16[2,1,64,1024]{3,1,2,0:T(2,128)(2,1)}, bf16[2,1,64,1024]{3,1,2,0:T(2,128)(2,1)}, u32[]{:S(2)}, u32[]{:S(2)}) collective-permute-start(bf16[2,1,64,1024]{3,1,2,0:T(2,128)(2,1)} %get-tuple-element.41), channel_id=1, source_target_pairs={{0,3},{1,4},{2,5},{3,6},{4,7},{5,8},{6,9},{7,10},{8,11},{9,12},{10... | collective-permute-start | bytes 786440 | tf_op jit(solution)/shard_map/ppermute | solution.py:16
  103.0 53.3 %collective-permute-start.6 = (bf16[2,1,64,1024]{3,1,2,0:T(2,128)(2,1)}, bf16[2,1,64,1024]{3,1,2,0:T(2,128)(2,1)}, u32[]{:S(2)}, u32[]{:S(2)}) collective-permute-start(bf16[2,1,64,1024]{3,1,2,0:T(2,128)(2,1)} %get-tuple-element.40), channel_id=1, source_target_pairs={{3,0},{4,1},{5,2},{6,3},{7,4},{8,5},{9,6},{10,7},{11,8},{12,9},{13... | collective-permute-start | bytes 786440 | tf_op jit(solution)/shard_map/ppermute | solution.py:16
  106.5 57.6 %collective-permute-start.7 = (bf16[2,1,64,1024]{3,1,2,0:T(2,128)(2,1)}, bf16[2,1,64,1024]{3,1,2,0:T(2,128)(2,1)}, u32[]{:S(2)}, u32[]{:S(2)}) collective-permute-start(bf16[2,1,64,1024]{3,1,2,0:T(2,128)(2,1)} %get-tuple-element.45), channel_id=1, source_target_pairs={{2,0},{3,1},{4,2},{5,3},{6,4},{7,5},{8,6},{9,7},{10,8},{11,9},{12,... | collective-permute-start | bytes 786440 | tf_op jit(solution)/shard_map/ppermute | solution.py:16
  109.4 67.0 %collective-permute-start.8 = (bf16[2,1,64,1024]{3,1,2,0:T(2,128)(2,1)}, bf16[2,1,64,1024]{3,1,2,0:T(2,128)(2,1)}, u32[]{:S(2)}, u32[]{:S(2)}) collective-permute-start(bf16[2,1,64,1024]{3,1,2,0:T(2,128)(2,1)} %get-tuple-element.44), channel_id=1, source_target_pairs={{1,0},{2,1},{3,2},{4,3},{5,4},{6,5},{7,6},{8,7},{9,8},{10,9},{11,1... | collective-permute-start | bytes 786440 | tf_op jit(solution)/shard_map/ppermute | solution.py:16
  112.4 0.8 copy-start.16
  113.2 63.2 %collective-permute-start.9 = (bf16[2,1,64,1024]{3,1,2,0:T(2,128)(2,1)}, bf16[2,1,64,1024]{3,1,2,0:T(2,128)(2,1)}, u32[]{:S(2)}, u32[]{:S(2)}) collective-permute-start(bf16[2,1,64,1024]{3,1,2,0:T(2,128)(2,1)} %get-tuple-element.43), channel_id=1, source_target_pairs={{0,1},{1,2},{2,3},{3,4},{4,5},{5,6},{6,7},{7,8},{8,9},{9,10},{10,1... | collective-permute-start | bytes 786440 | tf_op jit(solution)/shard_map/ppermute | solution.py:16
  127.7 53.4 %copy-start.12 = (bf16[2,1,64,512]{3,1,2,0:T(2,128)(2,1)S(1)}, bf16[2,1,64,512]{3,1,2,0:T(2,128)(2,1)}, u32[]{:S(2)}) copy-start(bf16[2,1,64,512]{3,1,2,0:T(2,128)(2,1)} %reshape.515) | copy-start | bytes 393220
  127.7 54.2 %copy-start.2 = (bf16[2,1,64,1024]{3,2,1,0:T(8,128)(2,1)S(1)}, bf16[2,1,64,1024]{3,2,1,0:T(8,128)(2,1)}, u32[]{:S(2)}) copy-start(bf16[2,1,64,1024]{3,2,1,0:T(8,128)(2,1)} %param.9) | copy-start | bytes 786436
  186.4 0.7 copy-start.10
  189.6 42.1 %all-to-all-start.2 = ((bf16[2,64,1,512]{3,0,2,1:T(2,128)(2,1)}), bf16[2,64,1,512]{3,0,2,1:T(2,128)(2,1)S(1)}, u32[]{:S(2)}, u32[]{:S(2)}) async-start(bf16[2,64,1,512]{3,0,2,1:T(2,128)(2,1)} %copy.396), calls=%async_computation.2 | async-start | bytes 262144 | tf_op jit(solution)/shard_map/all_to_all | solution.py:78
  231.7 34.1 %all-to-all-start = ((bf16[2,64,1,1536]{3,0,2,1:T(2,128)(2,1)}), bf16[2,64,1,1536]{3,0,2,1:T(2,128)(2,1)}, u32[]{:S(2)}, u32[]{:S(2)}) async-start(bf16[2,64,1,1536]{3,0,2,1:T(2,128)(2,1)} %copy.370), calls=%async_computation | async-start | bytes 786432 | tf_op jit(solution)/shard_map/all_to_all | solution.py:78
  275.9 2.1 copy-start.14
  275.9 2.1 copy-start.20
  275.9 2.1 copy-start.22
  281.5 23.2 %all-to-all-start.1 = ((bf16[2,1,64,512]{3,0,1,2:T(2,128)(2,1)}), bf16[2,1,64,512]{3,0,1,2:T(2,128)(2,1)S(1)}, u32[]{:S(2)}, u32[]{:S(2)}) async-start(bf16[2,1,64,512]{3,0,1,2:T(2,128)(2,1)} %copy.376), calls=%async_computation.1 | async-start | bytes 262144 | tf_op jit(solution)/shard_map/all_to_all | solution.py:82
  286.0 2.7 copy-start.11
  286.1 2.9 copy-start.15
  286.1 2.9 copy-start.21
  304.6 34.1 %all-to-all-start.3 = ((bf16[2,1,64,1536]{3,0,1,2:T(2,128)(2,1)}), bf16[2,1,64,1536]{3,0,1,2:T(2,128)(2,1)}, u32[]{:S(2)}, u32[]{:S(2)}) async-start(bf16[2,1,64,1536]{3,0,1,2:T(2,128)(2,1)} %reshape.518), calls=%async_computation.3 | async-start | bytes 786432 | tf_op jit(solution)/shard_map/all_to_all | solution.py:82
  312.1 31.8 %copy-start.3 = (bf16[2,1,64,1024]{3,2,0,1:T(8,128)(2,1)S(1)}, bf16[2,1,64,1024]{3,2,0,1:T(8,128)(2,1)}, u32[]{:S(2)}) copy-start(bf16[2,1,64,1024]{3,2,0,1:T(8,128)(2,1)} %get-tuple-element.54) | copy-start | bytes 786436
where the time goes:
time: 348 us; the launch traced here: 346 us
  waiting for transfers between devices  140 us (40%)
  starting transfers between devices  91.7 us (26%)
  local copies, waits for them, and re-layouts  57.3 us (16%)
  matrix products  36.8 us (11%)
  other arithmetic  18.1 us (5%)
    ppermute x12, waiting for transfers between devices, from_behind(): return lax.ppermute(block, axis, route)  60.8 us
    ppermute x12, starting transfers between devices, from_behind(): return lax.ppermute(block, axis, route)  53.2 us
    all_to_all x2, waiting for transfers between devices, to_frames(): lax.all_to_all(flipped, 'tm', split_axis=1, concat_axis=2, tiled=True)  41.6 us
    all_to_all x2, waiting for transfers between devices, to_patches(): back = lax.all_to_all(rows, 'tm', split_axis=2, concat_axis=1, tiled=True)  37.7 us
    all_to_all x2, starting transfers between devices, to_frames(): lax.all_to_all(flipped, 'tm', split_axis=1, concat_axis=2, tiled=True)  28.7 us
    dot_general x12, matrix products, contract(): return jnp.einsum(spec, left, right, preferred_element_type=jnp.float32)  14.5 us
    unnamed x57, local copies, waits for them, and re-layouts  14.1 us
    dot_general x4, matrix products, matmul_tr(): lax.dot_general(left, right, (((left.ndim - 1,), (1,)), ((), ())), prefer...  10.1 us
  transfers between devices with their start and end apart: 16, of which 10 were waited for; matrix products, arithmetic and copies ran while one was open for 9% of the time, Pallas kernels for 0%

commit v1 on v0

v1 whole, which is shorter than its diff:
```python
import functools

import jax
import jax.numpy as jnp
from jax import lax
from jax.experimental import pallas as pl
from jax.experimental.pallas import tpu as pltpu
from jax.sharding import PartitionSpec as P

HEADS = 8
HEAD_DIM = 64
INNER = HEADS * HEAD_DIM
EPSILON = 1e-05
FACTOR = HEAD_DIM ** (-0.5)
BF16 = jnp.bfloat16
F32 = jnp.float32


def normed(rows):
    values_f = rows.astype(F32)
    center = values_f - jnp.mean(values_f, -1, keepdims=True)
    inv_std = lax.rsqrt(jnp.mean(center * center, -1, keepdims=True) + EPSILON)
    return (center * inv_std, inv_std)


def norm_back(rows, grad_in):
    normal_rows, inv_std = normed(rows)
    return inv_std * (
        grad_in
        - jnp.mean(grad_in, -1, keepdims=True)
        - normal_rows * jnp.mean(grad_in * normal_rows, -1, keepdims=True)
    )


def mm(left, right):
    return jnp.dot(left, right, preferred_element_type=F32)


def mm_nt(left, right):
    return lax.dot_general(left, right, (((1,), (1,)), ((), ())), preferred_element_type=F32)


def mm_tn(left, right):
    return lax.dot_general(left, right, (((0,), (0,)), ((), ())), preferred_element_type=F32)


def low_lanes(shape):
    return lax.broadcasted_iota(jnp.int32, shape, len(shape) - 1) < HEAD_DIM


def split_halves(pair, low):
    zero = jnp.zeros_like(pair)
    return (jnp.where(low, pair, zero), jnp.where(low, zero, pair))


def softmax_grads(scores, weight_grad):
    top = jnp.max(scores, -1, keepdims=True)
    powers = jnp.exp(scores - top)
    weights = powers / jnp.sum(powers, -1, keepdims=True)
    row_delta = jnp.sum(weights * weight_grad, -1, keepdims=True)
    score_grad = (weights * (weight_grad - row_delta)).astype(BF16)
    return (weights.astype(BF16), score_grad)


def project_kernel(y_ref, grad_ref, qkv_ref, out_w_ref, send_ref):
    clips = send_ref.shape[0] // HEADS
    patches = send_ref.shape[1]
    normal, unused = normed(y_ref[...])
    proj = mm(normal.astype(BF16), qkv_ref[...])
    out_grad = mm_nt(grad_ref[...], out_w_ref[...])
    low = low_lanes((clips * patches, 2 * HEAD_DIM))
    for pair in range(HEADS // 2):
        cols = slice(2 * HEAD_DIM * pair, 2 * HEAD_DIM * (pair + 1))
        parts = [proj[:, INNER * i :][:, cols] for i in range(3)]
        queries, keys, values = parts
        grads = out_grad[:, cols]
        for half in range(2):
            tiles = []
            for left, right in ((queries, grads), (keys, values)):
                if half == 0:
                    tile = jnp.where(low, left, pltpu.roll(right, HEAD_DIM, 1))
                else:
                    tile = jnp.where(low, pltpu.roll(left, HEAD_DIM, 1), right)
                tiles.append(tile.astype(BF16))
            head = 2 * pair + half
            for clip in range(clips):
                rows = slice(patches * clip, patches * (clip + 1))
                for i in range(2):
                    send_ref[clip * HEADS + head, :, 128 * i : 128 * (i + 1)] = tiles[i][rows]


def space_kernel(pattern_ref, x_ref, out_ref, acc_ref):
    width = 2 * HEAD_DIM
    blocks = pattern_ref.shape[1]
    block = x_ref.shape[0] // blocks
    low_q = low_lanes((block, width))
    low_k = low_lanes((2 * block, width))
    scale = jnp.where(low_q, jnp.float32(FACTOR), jnp.float32(1.0))
    acc_ref[...] = jnp.zeros_like(acc_ref)
    for b in range(blocks):
        own = slice(block * b, block * (b + 1))
        beside = pl.ds(pl.multiple_of(pattern_ref[0, b] * block, block), block)
        query_rows = x_ref[own, :width]
        key_rows = jnp.concatenate([x_ref[own, width:], x_ref[beside, width:]], 0)
        q_low, g_high = split_halves(query_rows, low_q)
        k_low, v_high = split_halves(key_rows, low_k)
        stacked_q = jnp.concatenate([q_low, g_high], 0)
        both = mm_nt(stacked_q, key_rows)
        weights, score_grad = softmax_grads(both[:block] * FACTOR, both[block:])
        rows_out = mm(
            jnp.concatenate([score_grad, weights], 1), jnp.concatenate([k_low, v_high], 0)
        )
        out_ref[own, :width] = (rows_out * scale).astype(BF16)
        key_out = mm_tn(jnp.concatenate([score_grad, weights], 0), stacked_q)
        acc_ref[own, :] += key_out[:block]
        acc_ref[beside, :] += key_out[block:]
    for b in range(blocks):
        own = slice(block * b, block * (b + 1))
        out_ref[own, width:] = (acc_ref[own, :] * scale).astype(BF16)


def middle_kernel(
    recv_ref,
    y_first_ref,
    y_second_ref,
    grad_first_ref,
    space_qkv_ref,
    space_out_ref,
    time_out_ref,
    x_second_ref,
    dx_first_ref,
    send_ref,
):
    clips = recv_ref.shape[0] // HEADS
    patches = recv_ref.shape[1]
    low = low_lanes((patches, 2 * HEAD_DIM))
    sections = [[], [], [], []]
    for pair in range(HEADS // 2):
        made = [[], [], [], []]
        for clip in range(clips):
            at = clip * HEADS + 2 * pair
            for i in range(2):
                first = recv_ref[at, :, 128 * i : 128 * (i + 1)].astype(F32)
                second = recv_ref[at + 1, :, 128 * i : 128 * (i + 1)].astype(F32)
                made[2 * i].append(jnp.where(low, first, pltpu.roll(second, HEAD_DIM, 1)))
                made[2 * i + 1].append(jnp.where(low, pltpu.roll(first, HEAD_DIM, 1), second))
        for i in range(4):
            sections[i].append(jnp.concatenate(made[i], 0).astype(BF16))
    query_grad, mixed, key_grad, value_grad = [jnp.concatenate(s, 1) for s in sections]
    x_second = (y_second_ref[...].astype(F32) - mm(mixed, space_out_ref[...])).astype(BF16)
    x_second_ref[...] = x_second
    normal, unused = normed(x_second)
    send_ref[:, : x_second.shape[1]] = normal.astype(BF16)
    dqkv = jnp.concatenate([query_grad, key_grad, value_grad], 1)
    grad_in = mm_nt(dqkv, space_qkv_ref[...])
    dx_first = (
        grad_first_ref[...].astype(F32) + norm_back(y_first_ref[...], grad_in)
    ).astype(BF16)
    dx_first_ref[...] = dx_first
    send_ref[:, x_second.shape[1] :] = mm_nt(dx_first, time_out_ref[...]).astype(BF16)


def time_kernel(x_ref, qkv_ref, send_ref, *, sequences):
    rows = x_ref.shape[0]
    width = x_ref.shape[1] - INNER
    proj = mm(x_ref[:, :width], qkv_ref[...]).astype(BF16)
    lanes = 2 * HEAD_DIM
    low = low_lanes((rows, lanes))
    row_id = lax.broadcasted_iota(jnp.int32, (2 * rows, rows), 0)
    col_id = lax.broadcasted_iota(jnp.int32, (2 * rows, rows), 1)
    same = ((row_id ^ col_id) & (sequences - 1)) == 0
    lowest = jnp.finfo(jnp.float32).min
    sections = [[], [], []]
    for pair in range(HEADS // 2):
        at = lanes * pair
        queries = jnp.concatenate(split_halves(proj[:, at : at + lanes], low), 0)
        keys = proj[:, INNER + at : INNER + at + lanes]
        values = proj[:, 2 * INNER + at : 2 * INNER + at + lanes]
        grads = jnp.concatenate(
            split_halves(x_ref[:, width + at : width + at + lanes], low), 0
        )
        scores = jnp.where(same, mm_nt(queries, keys) * FACTOR, lowest)
        weights, score_grad = softmax_grads(scores, mm_nt(grads, values))
        keys_split = jnp.concatenate(split_halves(keys, low), 0)
        values_split = jnp.concatenate(split_halves(values, low), 0)
        mixed = mm(jnp.concatenate([weights[:rows], weights[rows:]], 1), values_split)
        send_ref[:, at : at + lanes] = mixed.astype(BF16)
        query_grad = mm(jnp.concatenate([score_grad[:rows], score_grad[rows:]], 1), keys_split)
        sections[0].append((query_grad * FACTOR).astype(BF16))
        sections[1].append((mm_tn(score_grad, queries) * FACTOR).astype(BF16))
        sections[2].append(mm_tn(weights, grads).astype(BF16))
    dqkv = jnp.concatenate(sections[0] + sections[1] + sections[2], 1)
    send_ref[:, INNER:] = mm_nt(dqkv, qkv_ref[...]).astype(BF16)


def last_kernel(recv_ref, y_first_ref, x_second_ref, grad_second_ref, out_w_ref, x_first_ref, dx_ref):
    value = mm(recv_ref[:, :INNER], out_w_ref[...])
    x_first_ref[...] = (y_first_ref[...].astype(F32) - value).astype(BF16)
    grad_in = recv_ref[:, INNER:].astype(F32)
    dx_ref[...] = (
        grad_second_ref[...].astype(F32) + norm_back(x_second_ref[...], grad_in)
    ).astype(BF16)


def shape_of(*sizes):
    return jax.ShapeDtypeStruct(sizes, BF16)


def exchange(rows, axis):
    return lax.all_to_all(rows, axis, split_axis=0, concat_axis=0, tiled=True)


def per_device(
    y_first, y_second, grad_first, grad_second, pattern, time_qkv, time_out, space_qkv, space_out
):
    shape = y_first.shape
    clips, unused, patches, width = shape
    rows = clips * patches
    flat = [a.reshape(rows, width) for a in (y_first, y_second, grad_first, grad_second)]
    y_first, y_second, grad_first, grad_second = flat
    groups = clips * HEADS
    head_cols = 4 * HEAD_DIM
    frames = lax.axis_size("tm")

    sent = pl.pallas_call(
        project_kernel, out_shape=shape_of(groups, patches, head_cols), name="project"
    )(y_first, grad_second, space_qkv, space_out)
    gathered = exchange(sent, "space").reshape(groups * patches, head_cols)
    space_rows = pl.pallas_call(
        space_kernel,
        out_shape=shape_of(groups * patches, head_cols),
        in_specs=[
            pl.BlockSpec(memory_space=pltpu.SMEM),
            pl.BlockSpec(memory_space=pltpu.VMEM),
        ],
        scratch_shapes=[pltpu.VMEM((groups * patches, 2 * HEAD_DIM), F32)],
        name="space_attention",
    )(pattern, gathered)
    returned = exchange(space_rows.reshape(groups, patches, head_cols), "space")
    x_second, dx_first, time_send = pl.pallas_call(
        middle_kernel,
        out_shape=(shape_of(rows, width), shape_of(rows, width), shape_of(rows, width + INNER)),
        name="middle",
    )(returned, y_first, y_second, grad_first, space_qkv, space_out, time_out)
    time_in = exchange(time_send.reshape(frames, rows // frames, width + INNER), "tm")
    time_rows = pl.pallas_call(
        functools.partial(time_kernel, sequences=rows // frames),
        out_shape=shape_of(rows, width + INNER),
        name="time_attention",
    )(time_in.reshape(rows, width + INNER), time_qkv)
    time_back = exchange(time_rows.reshape(frames, rows // frames, width + INNER), "tm")
    x_first, dx_second = pl.pallas_call(
        last_kernel, out_shape=(shape_of(rows, width), shape_of(rows, width)), name="last"
    )(time_back.reshape(rows, width + INNER), y_first, x_second, grad_second, time_out)
    return tuple(a.reshape(shape) for a in (x_first, x_second, dx_first, dx_second))


def solution(mesh):
    in_specs = (
        P(None, "tm", "space", None),
        P(None, "tm", "space", None),
        P(None, "tm", "space", None),
        P(None, "tm", "space", None),
        P("tm", None),
        P(),
        P(),
        P(),
        P(),
    )
    out_specs = (
        P(None, "tm", "space", None),
        P(None, "tm", "space", None),
        P(None, "tm", "space", None),
        P(None, "tm", "space", None),
    )
    return jax.shard_map(
        per_device, mesh=mesh, in_specs=in_specs, out_specs=out_specs, check_vma=False
    )
```

time: 348 us -> 157 us (0.45)
  the two profiles are of different devices: /device:TPU:25 before, /device:TPU:1 now
where the time goes in v1:
time: 157 us
  blocking collectives  128 us (82%)
  Pallas kernels  23.7 us (15%)
  local copies, waits for them, and re-layouts  4.07 us (3%)
    all_to_all x4, blocking collectives, exchange(): return lax.all_to_all(rows, axis, split_axis=0, concat_axis=0, tiled=True)  128 us
    pallas_call x1, Pallas kernels, per_device(): pl.pallas_call(functools.partial(time_kernel, sequences=rows // frames),...  6.12 us
    pallas_call x1, Pallas kernels, per_device(): pl.pallas_call(middle_kernel, out_shape=(shape_of(rows, width), shape_of(...  5.6 us
    pallas_call x1, Pallas kernels, per_device(): pl.pallas_call(space_kernel, out_shape=shape_of(groups * patches, head_co...  4.76 us
    pallas_call x1, Pallas kernels, per_device(): pl.pallas_call(project_kernel, out_shape=shape_of(groups, patches, head_c...  4.3 us

profile of v1, /device:TPU:1, one launch (start us, length us, event | category | flops | bytes accessed | tf_op | source)
XLA Modules:
  0.0 156.7 jit_solution(166690283935337836)
XLA Ops:
  0.6 4.3 %project.1 = bf16[16,64,256]{2,1,0:T(8,128)(2,1)} custom-call(bf16[128,1024]{1,0:T(8,128)(2,1)} %bitcast.18, bf16[128,1024]{1,0:T(8,128)(2,1)} %bitcast.23, bf16[1024,1536]{1,0:T(8,128)(2,1)} %space_qkv_ref.1, bf16[512,1024]{1,0:T(8,128)(2,1)} %space_out_ref.1), custom_call_target="tpu_custom_call" | custom-call | tf_op jit(solution)/shard_map/project/pallas_call | solution.py:225
  4.9 19.1 %all_to_all.20 = bf16[16,64,256]{2,1,0:T(8,128)(2,1)} all-to-all(bf16[16,64,256]{2,1,0:T(8,128)(2,1)} %project.1), channel_id=1, replica_groups=mesh['tm'=64,'space'=16] {'space'}, dimensions={0} | all-to-all | bytes 1048576 | tf_op jit(solution)/shard_map/all_to_all | solution.py:210
  24.0 4.8 %space_attention.1 = bf16[1024,256]{1,0:T(8,128)(2,1)} custom-call(s32[1,8]{1,0:T(1,128)} %pattern_ref.1, bf16[1024,256]{1,0:T(8,128)(2,1)} %bitcast.21), custom_call_target="tpu_custom_call" | custom-call | tf_op jit(solution)/shard_map/space_attention/pallas_call | solution.py:229
  28.8 14.7 %all_to_all.21.recv_ref = bf16[16,64,256]{2,1,0:T(8,128)(2,1)} all-to-all(bf16[16,64,256]{2,1,0:T(8,128)(2,1)} %bitcast.22), channel_id=1, replica_groups=mesh['tm'=64,'space'=16] {'space'}, dimensions={0} | all-to-all | bytes 1048576 | tf_op jit(solution)/shard_map/all_to_all | solution.py:210
  43.5 5.6 %middle.1 = (bf16[128,1024]{1,0:T(8,128)(2,1)}, bf16[128,1024]{1,0:T(8,128)(2,1)}, bf16[128,1536]{1,0:T(8,128)(2,1)}) custom-call(bf16[16,64,256]{2,1,0:T(8,128)(2,1)} %all_to_all.21.recv_ref, bf16[128,1024]{1,0:T(8,128)(2,1)} %bitcast.19, bf16[128,1024]{1,0:T(8,128)(2,1)} %bitcast.25, bf16[128,1024]{1,0:T(8,128)(2,1)} %bitcast.26, ...), custom_call_target="tpu_custom_call" | custom-call | tf_op jit(solution)/shard_map/middle/pallas_call | solution.py:240
  49.1 1.1 reshape.56
  50.2 61.4 %all_to_all.22 = bf16[64,2,1536]{2,1,0:T(2,128)(2,1)S(1)} all-to-all(bf16[64,2,1536]{2,1,0:T(2,128)(2,1)S(1)} %reshape.56), channel_id=1, replica_groups=mesh['tm'=64,'space'=16] {'tm'}, dimensions={0} | all-to-all | bytes 786432 | tf_op jit(solution)/shard_map/all_to_all | solution.py:210
  111.6 0.9 reshape.57.x_ref
  112.5 6.1 %time_attention.1 = bf16[128,1536]{1,0:T(8,128)(2,1)} custom-call(bf16[128,1536]{1,0:T(8,128)(2,1)} %reshape.57.x_ref, bf16[1024,1536]{1,0:T(8,128)(2,1)} %qkv_ref.3), custom_call_target="tpu_custom_call" | custom-call | tf_op jit(solution)/shard_map/time_attention/pallas_call | solution.py:246
  118.6 1.1 reshape.58
  119.8 33.2 %all_to_all.23 = bf16[64,2,1536]{2,1,0:T(2,128)(2,1)S(1)} all-to-all(bf16[64,2,1536]{2,1,0:T(2,128)(2,1)S(1)} %reshape.58), channel_id=1, replica_groups=mesh['tm'=64,'space'=16] {'tm'}, dimensions={0} | all-to-all | bytes 786432 | tf_op jit(solution)/shard_map/all_to_all | solution.py:210
  153.0 0.9 reshape.59.recv_ref
  153.9 2.9 %last.1 = (bf16[128,1024]{1,0:T(8,128)(2,1)}, bf16[128,1024]{1,0:T(8,128)(2,1)}) custom-call(bf16[128,1536]{1,0:T(8,128)(2,1)} %reshape.59.recv_ref, bf16[128,1024]{1,0:T(8,128)(2,1)} %bitcast.20, bf16[128,1024]{1,0:T(8,128)(2,1)} %get-tuple-element.10.x_second_ref, bf16[128,1024]{1,0:T(8,128)(2,1)} %bitcast.24, bf16[512,1024]{1,0:T(8,128)(2,1)} %out_w_ref.3), custom_call_target="tpu_custom_call" | custom-call | tf_op jit(solution)/shard_map/last/pallas_call | solution.py:252

commit v2 on v1

--- a/solution.py
+++ b/solution.py
@@ -1,5 +1,3 @@
-import functools
-
 import jax
 import jax.numpy as jnp
 from jax import lax
@@ -14,6 +12,7 @@
 FACTOR = HEAD_DIM ** (-0.5)
 BF16 = jnp.bfloat16
 F32 = jnp.float32
+PARAMS = pltpu.CompilerParams(vmem_limit_bytes=24 << 20)
 
 
 def normed(rows):
@@ -150,53 +149,57 @@
     x_second = (y_second_ref[...].astype(F32) - mm(mixed, space_out_ref[...])).astype(BF16)
     x_second_ref[...] = x_second
     normal, unused = normed(x_second)
-    send_ref[:, : x_second.shape[1]] = normal.astype(BF16)
     dqkv = jnp.concatenate([query_grad, key_grad, value_grad], 1)
     grad_in = mm_nt(dqkv, space_qkv_ref[...])
     dx_first = (
         grad_first_ref[...].astype(F32) + norm_back(y_first_ref[...], grad_in)
     ).astype(BF16)
     dx_first_ref[...] = dx_first
-    send_ref[:, x_second.shape[1] :] = mm_nt(dx_first, time_out_ref[...]).astype(BF16)
-
-
-def time_kernel(x_ref, qkv_ref, send_ref, *, sequences):
-    rows = x_ref.shape[0]
-    width = x_ref.shape[1] - INNER
-    proj = mm(x_ref[:, :width], qkv_ref[...]).astype(BF16)
+    time_grad = mm_nt(dx_first, time_out_ref[...]).astype(BF16)
+    send_rows = jnp.concatenate([normal.astype(BF16), time_grad], 1)
+    send_ref[...] = send_rows.reshape(send_ref.shape)
+
+
+def time_kernel(x_ref, qkv_ref, send_ref, flat_ref):
+    rows = x_ref.shape[0] * x_ref.shape[1]
+    width = x_ref.shape[2] - INNER
+    flat_ref[...] = x_ref[...].reshape(rows, width + INNER)
+    proj = mm(flat_ref[:, :width], qkv_ref[...]).astype(BF16)
     lanes = 2 * HEAD_DIM
     low = low_lanes((rows, lanes))
     row_id = lax.broadcasted_iota(jnp.int32, (2 * rows, rows), 0)
     col_id = lax.broadcasted_iota(jnp.int32, (2 * rows, rows), 1)
-    same = ((row_id ^ col_id) & (sequences - 1)) == 0
+    same = ((row_id ^ col_id) & (x_ref.shape[1] - 1)) == 0
     lowest = jnp.finfo(jnp.float32).min
-    sections = [[], [], []]
+    sections = [[], [], [], []]
     for pair in range(HEADS // 2):
         at = lanes * pair
         queries = jnp.concatenate(split_halves(proj[:, at : at + lanes], low), 0)
         keys = proj[:, INNER + at : INNER + at + lanes]
         values = proj[:, 2 * INNER + at : 2 * INNER + at + lanes]
         grads = jnp.concatenate(
-            split_halves(x_ref[:, width + at : width + at + lanes], low), 0
+            split_halves(flat_ref[:, width + at : width + at + lanes], low), 0
         )
         scores = jnp.where(same, mm_nt(queries, keys) * FACTOR, lowest)
         weights, score_grad = softmax_grads(scores, mm_nt(grads, values))
         keys_split = jnp.concatenate(split_halves(keys, low), 0)
         values_split = jnp.concatenate(split_halves(values, low), 0)
         mixed = mm(jnp.concatenate([weights[:rows], weights[rows:]], 1), values_split)
-        send_ref[:, at : at + lanes] = mixed.astype(BF16)
+        sections[3].append(mixed.astype(BF16))
         query_grad = mm(jnp.concatenate([score_grad[:rows], score_grad[rows:]], 1), keys_split)
         sections[0].append((query_grad * FACTOR).astype(BF16))
         sections[1].append((mm_tn(score_grad, queries) * FACTOR).astype(BF16))
         sections[2].append(mm_tn(weights, grads).astype(BF16))
     dqkv = jnp.concatenate(sections[0] + sections[1] + sections[2], 1)
-    send_ref[:, INNER:] = mm_nt(dqkv, qkv_ref[...]).astype(BF16)
+    grad_in = mm_nt(dqkv, qkv_ref[...]).astype(BF16)
+    send_ref[...] = jnp.concatenate(sections[3] + [grad_in], 1).reshape(send_ref.shape)
 
 
 def last_kernel(recv_ref, y_first_ref, x_second_ref, grad_second_ref, out_w_ref, x_first_ref, dx_ref):
-    value = mm(recv_ref[:, :INNER], out_w_ref[...])
+    received = recv_ref[...].reshape(y_first_ref.shape[0], recv_ref.shape[2])
+    value = mm(received[:, :INNER], out_w_ref[...])
     x_first_ref[...] = (y_first_ref[...].astype(F32) - value).astype(BF16)
-    grad_in = recv_ref[:, INNER:].astype(F32)
+    grad_in = received[:, INNER:].astype(F32)
     dx_ref[...] = (
         grad_second_ref[...].astype(F32) + norm_back(x_second_ref[...], grad_in)
     ).astype(BF16)
@@ -221,9 +224,10 @@
     groups = clips * HEADS
     head_cols = 4 * HEAD_DIM
     frames = lax.axis_size("tm")
+    wire = (frames, rows // frames, width + INNER)
 
     sent = pl.pallas_call(
-        project_kernel, out_shape=shape_of(groups, patches, head_cols), name="project"
+        project_kernel, out_shape=shape_of(groups, patches, head_cols), name="project", compiler_params=PARAMS
     )(y_first, grad_second, space_qkv, space_out)
     gathered = exchange(sent, "space").reshape(groups * patches, head_cols)
     space_rows = pl.pallas_call(
@@ -235,23 +239,28 @@
         ],
         scratch_shapes=[pltpu.VMEM((groups * patches, 2 * HEAD_DIM), F32)],
         name="space_attention",
+        compiler_params=PARAMS,
     )(pattern, gathered)
     returned = exchange(space_rows.reshape(groups, patches, head_cols), "space")
     x_second, dx_first, time_send = pl.pallas_call(
         middle_kernel,
-        out_shape=(shape_of(rows, width), shape_of(rows, width), shape_of(rows, width + INNER)),
+        out_shape=(shape_of(rows, width), shape_of(rows, width), shape_of(*wire)),
         name="middle",
+        compiler_params=PARAMS,
     )(returned, y_first, y_second, grad_first, space_qkv, space_out, time_out)
-    time_in = exchange(time_send.reshape(frames, rows // frames, width + INNER), "tm")
     time_rows = pl.pallas_call(
-        functools.partial(time_kernel, sequences=rows // frames),
-        out_shape=shape_of(rows, width + INNER),
+        time_kernel,
+        out_shape=shape_of(*wire),
+        scratch_shapes=[pltpu.VMEM((rows, width + INNER), BF16)],
         name="time_attention",
-    )(time_in.reshape(rows, width + INNER), time_qkv)
-    time_back = exchange(time_rows.reshape(frames, rows // frames, width + INNER), "tm")
+        compiler_params=PARAMS,
+    )(exchange(time_send, "tm"), time_qkv)
     x_first, dx_second = pl.pallas_call(
-        last_kernel, out_shape=(shape_of(rows, width), shape_of(rows, width)), name="last"
-    )(time_back.reshape(rows, width + INNER), y_first, x_second, grad_second, time_out)
+        last_kernel,
+        out_shape=(shape_of(rows, width), shape_of(rows, width)),
+        name="last",
+        compiler_params=PARAMS,
+    )(exchange(time_rows, "tm"), y_first, x_second, grad_second, time_out)
     return tuple(a.reshape(shape) for a in (x_first, x_second, dx_first, dx_second))
 
 

time: 157 us -> 146 us (0.930)
  Pallas kernels: 23.7 us -> 12 us
    unnamed x0 -> x28, local copies, waits for them, and re-layouts: none -> 5.05 us
    reshape x4 -> x0, local copies, waits for them, and re-layouts: 4.07 us -> none  [the longest x1 1.14 us: per_device(): time_send.reshape(frames, rows // frames, width + INNER)]
    pallas_call x1, Pallas kernels: 4.3 us -> 1.16 us  [per_device(): pl.pallas_call(project_kernel, out_shape=shape_of(groups, patches, head_c...]
    pallas_call x1, Pallas kernels: 5.6 us -> 2.53 us  [per_device(): pl.pallas_call(middle_kernel, out_shape=(shape_of(rows, width), shape_of(...]
    pallas_call x1, Pallas kernels: 6.12 us -> 3.35 us  [per_device(): pl.pallas_call(time_kernel, out_shape=shape_of(*wire), scratch_shapes=[pl...]
where the time goes in v2:
time: 146 us
  blocking collectives  128 us (88%)
  Pallas kernels  12 us (8%)
  local copies, waits for them, and re-layouts  5.05 us (3%)
    all_to_all x4, blocking collectives, exchange(): return lax.all_to_all(rows, axis, split_axis=0, concat_axis=0, tiled=True)  128 us
    unnamed x28, local copies, waits for them, and re-layouts  5.05 us
    pallas_call x1, Pallas kernels, per_device(): pl.pallas_call(space_kernel, out_shape=shape_of(groups * patches, head_co...  3.48 us
    pallas_call x1, Pallas kernels, per_device(): pl.pallas_call(time_kernel, out_shape=shape_of(*wire), scratch_shapes=[pl...  3.35 us

profile of v2, /device:TPU:1, one launch (start us, length us, event | category | flops | bytes accessed | tf_op | source)
XLA Modules:
  0.0 145.8 jit_solution(8888190890826792635)
XLA Ops:
  0.6 0.0 copy-start
  0.6 1.9 %copy-done = bf16[1024,1536]{1,0:T(8,128)(2,1)S(1)} copy-done((bf16[1024,1536]{1,0:T(8,128)(2,1)S(1)}, bf16[1024,1536]{1,0:T(8,128)(2,1)}, u32[]{:S(2)}) %copy-start) | copy-done | bytes 3145752
  2.5 0.0 copy-start.2
  2.5 1.2 copy-done.2
  3.7 0.0 copy-start.6
  3.8 0.9 copy-done.6
  4.7 0.0 copy-start.8
  4.7 0.9 copy-done.8
  5.7 0.0 copy-start.13
  5.7 0.0 copy-start.1
  5.7 0.0 copy-start.3
  5.7 0.0 copy-start.4
  5.7 0.0 copy-start.7
  5.7 0.0 copy-start.10
  5.7 0.0 copy-start.11
  5.7 1.2 project.1
  6.9 18.9 %all_to_all.20 = bf16[16,64,256]{2,1,0:T(8,128)(2,1)S(1)} all-to-all(bf16[16,64,256]{2,1,0:T(8,128)(2,1)S(1)} %project.1), channel_id=1, replica_groups=mesh['tm'=64,'space'=16] {'space'}, dimensions={0} | all-to-all | bytes 1048576 | tf_op jit(solution)/shard_map/all_to_all | solution.py:213
  25.8 0.0 copy-done.13
  25.8 3.5 %space_attention.1 = bf16[1024,256]{1,0:T(8,128)(2,1)S(1)} custom-call(s32[1,8]{1,0:T(1,128)S(1)} %copy-done.13, bf16[1024,256]{1,0:T(8,128)(2,1)S(1)} %bitcast.21), custom_call_target="tpu_custom_call" | custom-call | tf_op jit(solution)/shard_map/space_attention/pallas_call | solution.py:233
  29.2 14.4 %all_to_all.21.recv_ref = bf16[16,64,256]{2,1,0:T(8,128)(2,1)S(1)} all-to-all(bf16[16,64,256]{2,1,0:T(8,128)(2,1)S(1)} %bitcast.22), channel_id=1, replica_groups=mesh['tm'=64,'space'=16] {'space'}, dimensions={0} | all-to-all | bytes 1048576 | tf_op jit(solution)/shard_map/all_to_all | solution.py:213
  43.7 0.0 copy-done.1
  43.7 0.0 copy-done.3
  43.7 0.0 copy-done.4
  43.7 0.0 copy-done.7
  43.7 0.0 copy-done.10
  43.7 0.0 copy-done.11
  43.7 0.0 copy-start.5
  43.7 2.5 %middle.1 = (bf16[128,1024]{1,0:T(8,128)(2,1)}, bf16[128,1024]{1,0:T(8,128)(2,1)}, bf16[64,2,1536]{2,1,0:T(2,128)(2,1)S(1)}) custom-call(bf16[16,64,256]{2,1,0:T(8,128)(2,1)S(1)} %all_to_all.21.recv_ref, bf16[128,1024]{1,0:T(8,128)(2,1)S(1)} %bitcast.19, bf16[128,1024]{1,0:T(8,128)(2,1)S(1)} %bitcast.25, bf16[128,1024]{1,0:T(8,128)(2,1)S(1)} %bitcast.26, ...), custom_call_target="tpu_custom_call" | custom-call | tf_op jit(solution)/shard_map/middle/pallas_call | solution.py:245
  46.2 0.0 copy-start.9
  46.3 0.0 copy-start.12
  46.3 61.5 %all_to_all.22.x_ref = bf16[64,2,1536]{2,1,0:T(2,128)(2,1)S(1)} all-to-all(bf16[64,2,1536]{2,1,0:T(2,128)(2,1)S(1)} %get-tuple-element.9), channel_id=1, replica_groups=mesh['tm'=64,'space'=16] {'tm'}, dimensions={0} | all-to-all | bytes 786432 | tf_op jit(solution)/shard_map/all_to_all | solution.py:213
  107.8 0.0 copy-done.5
  107.8 3.3 %time_attention.1 = bf16[64,2,1536]{2,1,0:T(2,128)(2,1)S(1)} custom-call(bf16[64,2,1536]{2,1,0:T(2,128)(2,1)S(1)} %all_to_all.22.x_ref, bf16[1024,1536]{1,0:T(8,128)(2,1)S(1)} %copy-done.5), custom_call_target="tpu_custom_call" | custom-call | tf_op jit(solution)/shard_map/time_attention/pallas_call | solution.py:251
  111.1 33.2 %all_to_all.23.recv_ref = bf16[64,2,1536]{2,1,0:T(2,128)(2,1)S(1)} all-to-all(bf16[64,2,1536]{2,1,0:T(2,128)(2,1)S(1)} %time_attention.1), channel_id=1, replica_groups=mesh['tm'=64,'space'=16] {'tm'}, dimensions={0} | all-to-all | bytes 786432 | tf_op jit(solution)/shard_map/all_to_all | solution.py:213
  144.3 0.0 copy-done.9
  144.3 0.0 copy-done.12
  144.3 1.5 %last.1 = (bf16[128,1024]{1,0:T(8,128)(2,1)}, bf16[128,1024]{1,0:T(8,128)(2,1)}) custom-call(bf16[64,2,1536]{2,1,0:T(2,128)(2,1)S(1)} %all_to_all.23.recv_ref, bf16[128,1024]{1,0:T(8,128)(2,1)S(1)} %bitcast.20, bf16[128,1024]{1,0:T(8,128)(2,1)S(1)} %copy-done.12, bf16[128,1024]{1,0:T(8,128)(2,1)S(1)} %bitcast.24, bf16[512,1024]{1,0:T(8,128)(2,1)S(1)} %copy-done.4), custom_call_target="tpu_custom_call" | custom-call | tf_op jit(solution)/shard_map/last/pallas_call | solution.py:258
Async XLA Ops:
  0.6 1.9 %copy-start = (bf16[1024,1536]{1,0:T(8,128)(2,1)S(1)}, bf16[1024,1536]{1,0:T(8,128)(2,1)}, u32[]{:S(2)}) copy-start(bf16[1024,1536]{1,0:T(8,128)(2,1)} %space_qkv_ref.1) | copy-start | bytes 9437188
  2.5 1.2 copy-start.2
  3.7 0.9 copy-start.6
  4.7 0.9 copy-start.8
  5.7 20.1 %copy-start.13 = (s32[1,8]{1,0:T(1,128)S(1)}, s32[1,8]{1,0:T(1,128)}, u32[]{:S(2)}) copy-start(s32[1,8]{1,0:T(1,128)} %pattern_ref.1) | copy-start | bytes 100
  5.7 38.0 %copy-start.1 = (bf16[1024,1536]{1,0:T(8,128)(2,1)S(1)}, bf16[1024,1536]{1,0:T(8,128)(2,1)}, u32[]{:S(2)}) copy-start(bf16[1024,1536]{1,0:T(8,128)(2,1)} %space_qkv_ref.1) | copy-start | bytes 9437188
  5.7 38.0 %copy-start.3 = (bf16[512,1024]{1,0:T(8,128)(2,1)S(1)}, bf16[512,1024]{1,0:T(8,128)(2,1)}, u32[]{:S(2)}) copy-start(bf16[512,1024]{1,0:T(8,128)(2,1)} %space_out_ref.1) | copy-start | bytes 3145732
  5.7 38.0 %copy-start.4 = (bf16[512,1024]{1,0:T(8,128)(2,1)S(1)}, bf16[512,1024]{1,0:T(8,128)(2,1)}, u32[]{:S(2)}) copy-start(bf16[512,1024]{1,0:T(8,128)(2,1)} %out_w_ref.3) | copy-start | bytes 3145732
  5.7 38.0 %copy-start.7 = (bf16[2,1,64,1024]{3,2,1,0:T(8,128)(2,1)S(1)}, bf16[2,1,64,1024]{3,2,1,0:T(8,128)(2,1)}, u32[]{:S(2)}) copy-start(bf16[2,1,64,1024]{3,2,1,0:T(8,128)(2,1)} %param.9) | copy-start | bytes 786436
  5.7 38.0 %copy-start.10 = (bf16[2,1,64,1024]{3,2,1,0:T(8,128)(2,1)S(1)}, bf16[2,1,64,1024]{3,2,1,0:T(8,128)(2,1)}, u32[]{:S(2)}) copy-start(bf16[2,1,64,1024]{3,2,1,0:T(8,128)(2,1)} %param.10) | copy-start | bytes 786436
  5.7 38.0 %copy-start.11 = (bf16[2,1,64,1024]{3,2,1,0:T(8,128)(2,1)S(1)}, bf16[2,1,64,1024]{3,2,1,0:T(8,128)(2,1)}, u32[]{:S(2)}) copy-start(bf16[2,1,64,1024]{3,2,1,0:T(8,128)(2,1)} %param.11) | copy-start | bytes 786436
  43.7 64.1 %copy-start.5 = (bf16[1024,1536]{1,0:T(8,128)(2,1)S(1)}, bf16[1024,1536]{1,0:T(8,128)(2,1)}, u32[]{:S(2)}) copy-start(bf16[1024,1536]{1,0:T(8,128)(2,1)} %qkv_ref.3) | copy-start | bytes 9437188
  46.2 98.1 %copy-start.9 = (bf16[2,1,64,1024]{3,2,1,0:T(8,128)(2,1)S(1)}, bf16[2,1,64,1024]{3,2,1,0:T(8,128)(2,1)}, u32[]{:S(2)}) copy-start(bf16[2,1,64,1024]{3,2,1,0:T(8,128)(2,1)} %param.12) | copy-start | bytes 786436
  46.3 98.1 %copy-start.12 = (bf16[128,1024]{1,0:T(8,128)(2,1)S(1)}, bf16[128,1024]{1,0:T(8,128)(2,1)}, u32[]{:S(2)}) copy-start(bf16[128,1024]{1,0:T(8,128)(2,1)} %get-tuple-element.10.x_second_ref) | copy-start | bytes 786436

commit v3 on v2

--- a/solution.py
+++ b/solution.py
@@ -53,25 +53,42 @@
 
 
 def softmax_grads(scores, weight_grad):
-    top = jnp.max(scores, -1, keepdims=True)
+    top = jnp.max(scores, 0, keepdims=True)
     powers = jnp.exp(scores - top)
-    weights = powers / jnp.sum(powers, -1, keepdims=True)
-    row_delta = jnp.sum(weights * weight_grad, -1, keepdims=True)
+    weights = powers * (1.0 / jnp.sum(powers, 0, keepdims=True))
+    row_delta = jnp.sum(weights * weight_grad, 0, keepdims=True)
     score_grad = (weights * (weight_grad - row_delta)).astype(BF16)
     return (weights.astype(BF16), score_grad)
 
 
-def project_kernel(y_ref, grad_ref, qkv_ref, out_w_ref, send_ref):
+def project_kernel(
+    y_hbm, grad_hbm, qkv_hbm, out_w_hbm, send_ref, qkv_ref, out_w_ref, y_ref, grad_ref, sems
+):
     clips = send_ref.shape[0] // HEADS
     patches = send_ref.shape[1]
-    normal, unused = normed(y_ref[...])
-    proj = mm(normal.astype(BF16), qkv_ref[...])
+    pairs = [(y_hbm, y_ref), (grad_hbm, grad_ref), (out_w_hbm, out_w_ref)]
+    for i in range(3):
+        cols = pl.ds(INNER * i, INNER)
+        pairs.append((qkv_hbm.at[:, cols], qkv_ref.at[:, cols]))
+    copies = [
+        pltpu.make_async_copy(source, target, sems.at[i])
+        for i, (source, target) in enumerate(pairs)
+    ]
+    for copy in copies:
+        copy.start()
+    copies[0].wait()
+    normal = normed(y_ref[...])[0].astype(BF16)
+    copies[1].wait()
+    copies[2].wait()
     out_grad = mm_nt(grad_ref[...], out_w_ref[...])
+    proj = []
+    for i in range(3):
+        copies[3 + i].wait()
+        proj.append(mm(normal, qkv_ref[:, INNER * i : INNER * (i + 1)]))
     low = low_lanes((clips * patches, 2 * HEAD_DIM))
     for pair in range(HEADS // 2):
         cols = slice(2 * HEAD_DIM * pair, 2 * HEAD_DIM * (pair + 1))
-        parts = [proj[:, INNER * i :][:, cols] for i in range(3)]
-        queries, keys, values = parts
+        queries, keys, values = [part[:, cols] for part in proj]
         grads = out_grad[:, cols]
         for half in range(2):
             tiles = []
@@ -88,34 +105,50 @@
                     send_ref[clip * HEADS + head, :, 128 * i : 128 * (i + 1)] = tiles[i][rows]
 
 
-def space_kernel(pattern_ref, x_ref, out_ref, acc_ref):
+def space_kernel(pattern_ref, x_ref, out_ref, both_ref, grads_ref, own_ref, beside_ref):
     width = 2 * HEAD_DIM
     blocks = pattern_ref.shape[1]
     block = x_ref.shape[0] // blocks
     low_q = low_lanes((block, width))
     low_k = low_lanes((2 * block, width))
     scale = jnp.where(low_q, jnp.float32(FACTOR), jnp.float32(1.0))
-    acc_ref[...] = jnp.zeros_like(acc_ref)
+
+    def rows_of(b):
+        return slice(block * b, block * (b + 1))
+
+    def stacked_queries(b):
+        return jnp.concatenate(split_halves(x_ref[rows_of(b), :width], low_q), 0)
+
+    def key_rows(b):
+        beside = pl.ds(pl.multiple_of(pattern_ref[0, b] * block, block), block)
+        return jnp.concatenate([x_ref[rows_of(b), width:], x_ref[beside, width:]], 0)
+
+    def score(b):
+        both_ref[b] = mm_nt(key_rows(b), stacked_queries(b))
+
+    def weigh(b):
+        weights, score_grad = softmax_grads(both_ref[b, :, :block] * FACTOR, both_ref[b, :, block:])
+        grads_ref[b, :, :block] = score_grad
+        grads_ref[b, :, block:] = weights
+
+    def spread(b):
+        k_low, v_high = split_halves(key_rows(b), low_k)
+        rows_out = mm_tn(grads_ref[b, :, :block], k_low) + mm_tn(grads_ref[b, :, block:], v_high)
+        out_ref[rows_of(b), :width] = (rows_out * scale).astype(BF16)
+        key_out = mm(grads_ref[b], stacked_queries(b))
+        own_ref[rows_of(b), :] = key_out[:block]
+        beside_ref[rows_of(b), :] = key_out[block:]
+
+    for step in range(blocks + 2):
+        for stage, lag in ((score, 0), (weigh, 1), (spread, 2)):
+            if 0 <= step - lag < blocks:
+                stage(step - lag)
     for b in range(blocks):
-        own = slice(block * b, block * (b + 1))
-        beside = pl.ds(pl.multiple_of(pattern_ref[0, b] * block, block), block)
-        query_rows = x_ref[own, :width]
-        key_rows = jnp.concatenate([x_ref[own, width:], x_ref[beside, width:]], 0)
-        q_low, g_high = split_halves(query_rows, low_q)
-        k_low, v_high = split_halves(key_rows, low_k)
-        stacked_q = jnp.concatenate([q_low, g_high], 0)
-        both = mm_nt(stacked_q, key_rows)
-        weights, score_grad = softmax_grads(both[:block] * FACTOR, both[block:])
-        rows_out = mm(
-            jnp.concatenate([score_grad, weights], 1), jnp.concatenate([k_low, v_high], 0)
-        )
-        out_ref[own, :width] = (rows_out * scale).astype(BF16)
-        key_out = mm_tn(jnp.concatenate([score_grad, weights], 0), stacked_q)
-        acc_ref[own, :] += key_out[:block]
-        acc_ref[beside, :] += key_out[block:]
-    for b in range(blocks):
-        own = slice(block * b, block * (b + 1))
-        out_ref[own, width:] = (acc_ref[own, :] * scale).astype(BF16)
+        total = own_ref[rows_of(b), :]
+        for other in range(max(b - 1, 0), min(b + 2, blocks)):
+            part = beside_ref[rows_of(other), :]
+            total = total + jnp.where(pattern_ref[0, other] == b, part, 0.0)
+        out_ref[rows_of(b), width:] = (total * scale).astype(BF16)
 
 
 def middle_kernel(
@@ -167,8 +200,8 @@
     proj = mm(flat_ref[:, :width], qkv_ref[...]).astype(BF16)
     lanes = 2 * HEAD_DIM
     low = low_lanes((rows, lanes))
-    row_id = lax.broadcasted_iota(jnp.int32, (2 * rows, rows), 0)
-    col_id = lax.broadcasted_iota(jnp.int32, (2 * rows, rows), 1)
+    row_id = lax.broadcasted_iota(jnp.int32, (rows, 2 * rows), 0)
+    col_id = lax.broadcasted_iota(jnp.int32, (rows, 2 * rows), 1)
     same = ((row_id ^ col_id) & (x_ref.shape[1] - 1)) == 0
     lowest = jnp.finfo(jnp.float32).min
     sections = [[], [], [], []]
@@ -180,16 +213,18 @@
         grads = jnp.concatenate(
             split_halves(flat_ref[:, width + at : width + at + lanes], low), 0
         )
-        scores = jnp.where(same, mm_nt(queries, keys) * FACTOR, lowest)
-        weights, score_grad = softmax_grads(scores, mm_nt(grads, values))
+        scores = jnp.where(same, mm_nt(keys, queries) * FACTOR, lowest)
+        weights, score_grad = softmax_grads(scores, mm_nt(values, grads))
         keys_split = jnp.concatenate(split_halves(keys, low), 0)
         values_split = jnp.concatenate(split_halves(values, low), 0)
-        mixed = mm(jnp.concatenate([weights[:rows], weights[rows:]], 1), values_split)
+        mixed = mm_tn(jnp.concatenate([weights[:, :rows], weights[:, rows:]], 0), values_split)
         sections[3].append(mixed.astype(BF16))
-        query_grad = mm(jnp.concatenate([score_grad[:rows], score_grad[rows:]], 1), keys_split)
+        query_grad = mm_tn(
+            jnp.concatenate([score_grad[:, :rows], score_grad[:, rows:]], 0), keys_split
+        )
         sections[0].append((query_grad * FACTOR).astype(BF16))
-        sections[1].append((mm_tn(score_grad, queries) * FACTOR).astype(BF16))
-        sections[2].append(mm_tn(weights, grads).astype(BF16))
+        sections[1].append((mm(score_grad, queries) * FACTOR).astype(BF16))
+        sections[2].append(mm(weights, grads).astype(BF16))
     dqkv = jnp.concatenate(sections[0] + sections[1] + sections[2], 1)
     grad_in = mm_nt(dqkv, qkv_ref[...]).astype(BF16)
     send_ref[...] = jnp.concatenate(sections[3] + [grad_in], 1).reshape(send_ref.shape)
@@ -223,12 +258,33 @@
     y_first, y_second, grad_first, grad_second = flat
     groups = clips * HEADS
     head_cols = 4 * HEAD_DIM
+    blocks = pattern.shape[1]
+    block = groups * patches // blocks
     frames = lax.axis_size("tm")
     wire = (frames, rows // frames, width + INNER)
 
-    sent = pl.pallas_call(
-        project_kernel, out_shape=shape_of(groups, patches, head_cols), name="project", compiler_params=PARAMS
-    )(y_first, grad_second, space_qkv, space_out)
+    hbm = pl.BlockSpec(memory_space=pltpu.HBM)
+    sent, space_qkv, space_out = pl.pallas_call(
+        project_kernel,
+        out_shape=(
+            shape_of(groups, patches, head_cols),
+            shape_of(*space_qkv.shape),
+            shape_of(*space_out.shape),
+        ),
+        in_specs=[hbm] * 4,
+        scratch_shapes=[
+            pltpu.VMEM((rows, width), BF16),
+            pltpu.VMEM((rows, width), BF16),
+            pltpu.SemaphoreType.DMA((6,)),
+        ],
+        name="project",
+        compiler_params=PARAMS,
+    )(
+        *[
+            pltpu.with_memory_space_constraint(a, pltpu.HBM)
+            for a in (y_first, grad_second, space_qkv, space_out)
+        ]
+    )
     gathered = exchange(sent, "space").reshape(groups * patches, head_cols)
     space_rows = pl.pallas_call(
         space_kernel,
@@ -237,7 +293,12 @@
             pl.BlockSpec(memory_space=pltpu.SMEM),
             pl.BlockSpec(memory_space=pltpu.VMEM),
         ],
-        scratch_shapes=[pltpu.VMEM((groups * patches, 2 * HEAD_DIM), F32)],
+        scratch_shapes=[
+            pltpu.VMEM((blocks, 2 * block, 2 * block), F32),
+            pltpu.VMEM((blocks, 2 * block, 2 * block), BF16),
+            pltpu.VMEM((groups * patches, 2 * HEAD_DIM), F32),
+            pltpu.VMEM((groups * patches, 2 * HEAD_DIM), F32),
+        ],
         name="space_attention",
         compiler_params=PARAMS,
     )(pattern, gathered)

time: 146 us -> 141 us (0.966)
  local copies, waits for them, and re-layouts: 5.05 us -> 0.03 us
    unnamed x28 -> x16, local copies, waits for them, and re-layouts: 5.05 us -> 0.03 us
    pallas_call x1, Pallas kernels: 1.16 us -> 3.05 us  [per_device(): pl.pallas_call(project_kernel, out_shape=(shape_of(groups, patches, head_...]
where the time goes in v3:
time: 141 us
  blocking collectives  128 us (91%)
  Pallas kernels  12.1 us (9%)
    all_to_all x4, blocking collectives, exchange(): return lax.all_to_all(rows, axis, split_axis=0, concat_axis=0, tiled=True)  128 us
    pallas_call x1, Pallas kernels, per_device(): pl.pallas_call(project_kernel, out_shape=(shape_of(groups, patches, head_...  3.05 us

profile of v3, /device:TPU:1, one launch (start us, length us, event | category | flops | bytes accessed | tf_op | source)
XLA Modules:
  0.0 140.8 jit_solution(3309568337148440633)
XLA Ops:
  0.6 0.0 copy-start.7
  0.6 0.0 copy-start
  0.7 0.0 copy-start.2
  0.7 0.0 copy-start.4
  0.7 0.0 copy-start.5
  0.7 3.1 %project.1 = (bf16[16,64,256]{2,1,0:T(8,128)(2,1)S(1)}, bf16[1024,1536]{1,0:T(8,128)(2,1)S(1)}, bf16[512,1024]{1,0:T(8,128)(2,1)S(1)}) custom-call(bf16[128,1024]{1,0:T(8,128)(2,1)} %bitcast.18, bf16[128,1024]{1,0:T(8,128)(2,1)} %bitcast.23, bf16[1024,1536]{1,0:T(8,128)(2,1)} %qkv_hbm.1, bf16[512,1024]{1,0:T(8,128)(2,1)} %out_w_hbm.1), custom_call_target="tpu_custom_call" | custom-call | tf_op jit(solution)/shard_map/project/pallas_call | solution.py:267
  3.7 18.8 %all_to_all.20 = bf16[16,64,256]{2,1,0:T(8,128)(2,1)S(1)} all-to-all(bf16[16,64,256]{2,1,0:T(8,128)(2,1)S(1)} %get-tuple-element.12), channel_id=1, replica_groups=mesh['tm'=64,'space'=16] {'space'}, dimensions={0} | all-to-all | bytes 1048576 | tf_op jit(solution)/shard_map/all_to_all | solution.py:248
  22.5 0.0 copy-done.7
  22.5 2.2 %space_attention.1 = bf16[1024,256]{1,0:T(8,128)(2,1)S(1)} custom-call(s32[1,8]{1,0:T(1,128)S(1)} %copy-done.7, bf16[1024,256]{1,0:T(8,128)(2,1)S(1)} %bitcast.21), custom_call_target="tpu_custom_call" | custom-call | tf_op jit(solution)/shard_map/space_attention/pallas_call | solution.py:289
  24.7 14.4 %all_to_all.21.recv_ref = bf16[16,64,256]{2,1,0:T(8,128)(2,1)S(1)} all-to-all(bf16[16,64,256]{2,1,0:T(8,128)(2,1)S(1)} %bitcast.22), channel_id=1, replica_groups=mesh['tm'=64,'space'=16] {'space'}, dimensions={0} | all-to-all | bytes 1048576 | tf_op jit(solution)/shard_map/all_to_all | solution.py:248
  39.1 0.0 copy-done
  39.2 0.0 copy-done.2
  39.2 0.0 copy-done.4
  39.2 0.0 copy-done.5
  39.2 0.0 copy-start.1
  39.2 2.5 %middle.1 = (bf16[128,1024]{1,0:T(8,128)(2,1)}, bf16[128,1024]{1,0:T(8,128)(2,1)}, bf16[64,2,1536]{2,1,0:T(2,128)(2,1)S(1)}) custom-call(bf16[16,64,256]{2,1,0:T(8,128)(2,1)S(1)} %all_to_all.21.recv_ref, bf16[128,1024]{1,0:T(8,128)(2,1)S(1)} %bitcast.19, bf16[128,1024]{1,0:T(8,128)(2,1)S(1)} %bitcast.25, bf16[128,1024]{1,0:T(8,128)(2,1)S(1)} %bitcast.26, ...), custom_call_target="tpu_custom_call" | custom-call | tf_op jit(solution)/shard_map/middle/pallas_call | solution.py:306
  41.7 0.0 copy-start.3
  41.7 0.0 copy-start.6
  41.7 61.5 %all_to_all.22.x_ref = bf16[64,2,1536]{2,1,0:T(2,128)(2,1)S(1)} all-to-all(bf16[64,2,1536]{2,1,0:T(2,128)(2,1)S(1)} %get-tuple-element.15), channel_id=1, replica_groups=mesh['tm'=64,'space'=16] {'tm'}, dimensions={0} | all-to-all | bytes 786432 | tf_op jit(solution)/shard_map/all_to_all | solution.py:248
  103.2 0.0 copy-done.1
  103.2 2.8 %time_attention.1 = bf16[64,2,1536]{2,1,0:T(2,128)(2,1)S(1)} custom-call(bf16[64,2,1536]{2,1,0:T(2,128)(2,1)S(1)} %all_to_all.22.x_ref, bf16[1024,1536]{1,0:T(8,128)(2,1)S(1)} %copy-done.1), custom_call_target="tpu_custom_call" | custom-call | tf_op jit(solution)/shard_map/time_attention/pallas_call | solution.py:312
  106.0 33.2 %all_to_all.23.recv_ref = bf16[64,2,1536]{2,1,0:T(2,128)(2,1)S(1)} all-to-all(bf16[64,2,1536]{2,1,0:T(2,128)(2,1)S(1)} %time_attention.1), channel_id=1, replica_groups=mesh['tm'=64,'space'=16] {'tm'}, dimensions={0} | all-to-all | bytes 786432 | tf_op jit(solution)/shard_map/all_to_all | solution.py:248
  139.2 0.0 copy-done.3
  139.2 0.0 copy-done.6
  139.2 1.5 %last.1 = (bf16[128,1024]{1,0:T(8,128)(2,1)}, bf16[128,1024]{1,0:T(8,128)(2,1)}) custom-call(bf16[64,2,1536]{2,1,0:T(2,128)(2,1)S(1)} %all_to_all.23.recv_ref, bf16[128,1024]{1,0:T(8,128)(2,1)S(1)} %bitcast.20, bf16[128,1024]{1,0:T(8,128)(2,1)S(1)} %copy-done.6, bf16[128,1024]{1,0:T(8,128)(2,1)S(1)} %bitcast.24, bf16[512,1024]{1,0:T(8,128)(2,1)S(1)} %copy-done), custom_call_target="tpu_custom_call" | custom-call | tf_op jit(solution)/shard_map/last/pallas_call | solution.py:319
Async XLA Ops:
  0.6 21.9 %copy-start.7 = (s32[1,8]{1,0:T(1,128)S(1)}, s32[1,8]{1,0:T(1,128)}, u32[]{:S(2)}) copy-start(s32[1,8]{1,0:T(1,128)} %pattern_ref.1) | copy-start | bytes 100
  0.6 38.5 %copy-start = (bf16[512,1024]{1,0:T(8,128)(2,1)S(1)}, bf16[512,1024]{1,0:T(8,128)(2,1)}, u32[]{:S(2)}) copy-start(bf16[512,1024]{1,0:T(8,128)(2,1)} %out_w_ref.1) | copy-start | bytes 3145732
  0.7 38.5 %copy-start.2 = (bf16[2,1,64,1024]{3,2,1,0:T(8,128)(2,1)S(1)}, bf16[2,1,64,1024]{3,2,1,0:T(8,128)(2,1)}, u32[]{:S(2)}) copy-start(bf16[2,1,64,1024]{3,2,1,0:T(8,128)(2,1)} %param.9) | copy-start | bytes 786436
  0.7 38.5 %copy-start.4 = (bf16[2,1,64,1024]{3,2,1,0:T(8,128)(2,1)S(1)}, bf16[2,1,64,1024]{3,2,1,0:T(8,128)(2,1)}, u32[]{:S(2)}) copy-start(bf16[2,1,64,1024]{3,2,1,0:T(8,128)(2,1)} %param.10) | copy-start | bytes 786436
  0.7 38.5 %copy-start.5 = (bf16[2,1,64,1024]{3,2,1,0:T(8,128)(2,1)S(1)}, bf16[2,1,64,1024]{3,2,1,0:T(8,128)(2,1)}, u32[]{:S(2)}) copy-start(bf16[2,1,64,1024]{3,2,1,0:T(8,128)(2,1)} %param.11) | copy-start | bytes 786436
  39.2 64.1 %copy-start.1 = (bf16[1024,1536]{1,0:T(8,128)(2,1)S(1)}, bf16[1024,1536]{1,0:T(8,128)(2,1)}, u32[]{:S(2)}) copy-start(bf16[1024,1536]{1,0:T(8,128)(2,1)} %qkv_ref.1) | copy-start | bytes 9437188
  41.7 97.5 %copy-start.3 = (bf16[2,1,64,1024]{3,2,1,0:T(8,128)(2,1)S(1)}, bf16[2,1,64,1024]{3,2,1,0:T(8,128)(2,1)}, u32[]{:S(2)}) copy-start(bf16[2,1,64,1024]{3,2,1,0:T(8,128)(2,1)} %param.12) | copy-start | bytes 786436
  41.7 97.5 %copy-start.6 = (bf16[128,1024]{1,0:T(8,128)(2,1)S(1)}, bf16[128,1024]{1,0:T(8,128)(2,1)}, u32[]{:S(2)}) copy-start(bf16[128,1024]{1,0:T(8,128)(2,1)} %get-tuple-element.16.x_second_ref) | copy-start | bytes 786436

commit v4 on v3

--- a/solution.py
+++ b/solution.py
@@ -22,8 +22,7 @@
     return (center * inv_std, inv_std)
 
 
-def norm_back(rows, grad_in):
-    normal_rows, inv_std = normed(rows)
+def norm_back(normal_rows, inv_std, grad_in):
     return inv_std * (
         grad_in
         - jnp.mean(grad_in, -1, keepdims=True)
@@ -62,7 +61,18 @@
 
 
 def project_kernel(
-    y_hbm, grad_hbm, qkv_hbm, out_w_hbm, send_ref, qkv_ref, out_w_ref, y_ref, grad_ref, sems
+    y_hbm,
+    grad_hbm,
+    qkv_hbm,
+    out_w_hbm,
+    send_ref,
+    qkv_ref,
+    out_w_ref,
+    normal_ref,
+    std_ref,
+    y_ref,
+    grad_ref,
+    sems,
 ):
     clips = send_ref.shape[0] // HEADS
     patches = send_ref.shape[1]
@@ -77,32 +87,37 @@
     for copy in copies:
         copy.start()
     copies[0].wait()
-    normal = normed(y_ref[...])[0].astype(BF16)
+    normal, inv_std = normed(y_ref[...])
+    normal_ref[...] = normal
+    std_ref[...] = jnp.broadcast_to(inv_std, std_ref.shape)
+    normal = normal.astype(BF16)
     copies[1].wait()
     copies[2].wait()
     out_grad = mm_nt(grad_ref[...], out_w_ref[...])
-    proj = []
-    for i in range(3):
+    low = low_lanes((clips * patches, 2 * HEAD_DIM))
+
+    def assemble(lefts, rights, part):
+        for pair in range(HEADS // 2):
+            cols = slice(2 * HEAD_DIM * pair, 2 * HEAD_DIM * (pair + 1))
+            left, right = lefts[:, cols], rights[:, cols]
+            tiles = (
+                jnp.where(low, left, pltpu.roll(right, HEAD_DIM, 1)),
+                jnp.where(low, pltpu.roll(left, HEAD_DIM, 1), right),
+            )
+            for half in range(2):
+                tile = tiles[half].astype(BF16)
+                for clip in range(clips):
+                    send_ref[clip * HEADS + 2 * pair + half, :, 128 * part : 128 * (part + 1)] = (
+                        tile[patches * clip : patches * (clip + 1)]
+                    )
+
+    def projected(i):
         copies[3 + i].wait()
-        proj.append(mm(normal, qkv_ref[:, INNER * i : INNER * (i + 1)]))
-    low = low_lanes((clips * patches, 2 * HEAD_DIM))
-    for pair in range(HEADS // 2):
-        cols = slice(2 * HEAD_DIM * pair, 2 * HEAD_DIM * (pair + 1))
-        queries, keys, values = [part[:, cols] for part in proj]
-        grads = out_grad[:, cols]
-        for half in range(2):
-            tiles = []
-            for left, right in ((queries, grads), (keys, values)):
-                if half == 0:
-                    tile = jnp.where(low, left, pltpu.roll(right, HEAD_DIM, 1))
-                else:
-                    tile = jnp.where(low, pltpu.roll(left, HEAD_DIM, 1), right)
-                tiles.append(tile.astype(BF16))
-            head = 2 * pair + half
-            for clip in range(clips):
-                rows = slice(patches * clip, patches * (clip + 1))
-                for i in range(2):
-                    send_ref[clip * HEADS + head, :, 128 * i : 128 * (i + 1)] = tiles[i][rows]
+        return mm(normal, qkv_ref[:, INNER * i : INNER * (i + 1)])
+
+    assemble(projected(0), out_grad, 0)
+    keys = projected(1)
+    assemble(keys, projected(2), 1)
 
 
 def space_kernel(pattern_ref, x_ref, out_ref, both_ref, grads_ref, own_ref, beside_ref):
@@ -153,7 +168,8 @@
 
 def middle_kernel(
     recv_ref,
-    y_first_ref,
+    normal_first_ref,
+    std_first_ref,
     y_second_ref,
     grad_first_ref,
     space_qkv_ref,
@@ -162,6 +178,8 @@
     x_second_ref,
     dx_first_ref,
     send_ref,
+    normal_ref,
+    std_ref,
 ):
     clips = recv_ref.shape[0] // HEADS
     patches = recv_ref.shape[1]
@@ -181,63 +199,88 @@
     query_grad, mixed, key_grad, value_grad = [jnp.concatenate(s, 1) for s in sections]
     x_second = (y_second_ref[...].astype(F32) - mm(mixed, space_out_ref[...])).astype(BF16)
     x_second_ref[...] = x_second
-    normal, unused = normed(x_second)
+    normal, inv_std = normed(x_second)
+    normal_ref[...] = normal
+    std_ref[...] = jnp.broadcast_to(inv_std, std_ref.shape)
     dqkv = jnp.concatenate([query_grad, key_grad, value_grad], 1)
     grad_in = mm_nt(dqkv, space_qkv_ref[...])
-    dx_first = (
-        grad_first_ref[...].astype(F32) + norm_back(y_first_ref[...], grad_in)
-    ).astype(BF16)
+    grad_in = norm_back(normal_first_ref[...], std_first_ref[:, :1], grad_in)
+    dx_first = (grad_first_ref[...].astype(F32) + grad_in).astype(BF16)
     dx_first_ref[...] = dx_first
     time_grad = mm_nt(dx_first, time_out_ref[...]).astype(BF16)
     send_rows = jnp.concatenate([normal.astype(BF16), time_grad], 1)
     send_ref[...] = send_rows.reshape(send_ref.shape)
 
 
-def time_kernel(x_ref, qkv_ref, send_ref, flat_ref):
+def time_kernel(x_ref, qkv_ref, send_ref, flat_ref, proj_ref, both_ref, grads_ref, dqkv_ref):
     rows = x_ref.shape[0] * x_ref.shape[1]
     width = x_ref.shape[2] - INNER
     flat_ref[...] = x_ref[...].reshape(rows, width + INNER)
-    proj = mm(flat_ref[:, :width], qkv_ref[...]).astype(BF16)
+    for i in range(3):
+        cols = slice(INNER * i, INNER * (i + 1))
+        proj_ref[:, cols] = mm(flat_ref[:, :width], qkv_ref[:, cols]).astype(BF16)
     lanes = 2 * HEAD_DIM
     low = low_lanes((rows, lanes))
     row_id = lax.broadcasted_iota(jnp.int32, (rows, 2 * rows), 0)
     col_id = lax.broadcasted_iota(jnp.int32, (rows, 2 * rows), 1)
     same = ((row_id ^ col_id) & (x_ref.shape[1] - 1)) == 0
     lowest = jnp.finfo(jnp.float32).min
-    sections = [[], [], [], []]
-    for pair in range(HEADS // 2):
+    pairs = HEADS // 2
+    mixed_parts = []
+
+    def split_rows(ref, start, pair):
+        at = start + lanes * pair
+        return jnp.concatenate(split_halves(ref[:, at : at + lanes], low), 0)
+
+    def score(pair):
         at = lanes * pair
-        queries = jnp.concatenate(split_halves(proj[:, at : at + lanes], low), 0)
-        keys = proj[:, INNER + at : INNER + at + lanes]
-        values = proj[:, 2 * INNER + at : 2 * INNER + at + lanes]
-        grads = jnp.concatenate(
-            split_halves(flat_ref[:, width + at : width + at + lanes], low), 0
+        keys = proj_ref[:, INNER + at : INNER + at + lanes]
+        values = proj_ref[:, 2 * INNER + at : 2 * INNER + at + lanes]
+        both_ref[pair, :, : 2 * rows] = mm_nt(keys, split_rows(proj_ref, 0, pair))
+        both_ref[pair, :, 2 * rows :] = mm_nt(values, split_rows(flat_ref, width, pair))
+
+    def weigh(pair):
+        scores = jnp.where(same, both_ref[pair, :, : 2 * rows] * FACTOR, lowest)
+        weights, score_grad = softmax_grads(scores, both_ref[pair, :, 2 * rows :])
+        grads_ref[pair, :, : 2 * rows] = score_grad
+        grads_ref[pair, :, 2 * rows :] = weights
+
+    def spread(pair):
+        at = lanes * pair
+        score_grad = grads_ref[pair, :, : 2 * rows]
+        weights = grads_ref[pair, :, 2 * rows :]
+        mixed = mm_tn(
+            jnp.concatenate([weights[:, :rows], weights[:, rows:]], 0),
+            split_rows(proj_ref, 2 * INNER, pair),
         )
-        scores = jnp.where(same, mm_nt(keys, queries) * FACTOR, lowest)
-        weights, score_grad = softmax_grads(scores, mm_nt(values, grads))
-        keys_split = jnp.concatenate(split_halves(keys, low), 0)
-        values_split = jnp.concatenate(split_halves(values, low), 0)
-        mixed = mm_tn(jnp.concatenate([weights[:, :rows], weights[:, rows:]], 0), values_split)
-        sections[3].append(mixed.astype(BF16))
+        mixed_parts.append(mixed.astype(BF16))
         query_grad = mm_tn(
-            jnp.concatenate([score_grad[:, :rows], score_grad[:, rows:]], 0), keys_split
+            jnp.concatenate([score_grad[:, :rows], score_grad[:, rows:]], 0),
+            split_rows(proj_ref, INNER, pair),
         )
-        sections[0].append((query_grad * FACTOR).astype(BF16))
-        sections[1].append((mm(score_grad, queries) * FACTOR).astype(BF16))
-        sections[2].append(mm(weights, grads).astype(BF16))
-    dqkv = jnp.concatenate(sections[0] + sections[1] + sections[2], 1)
-    grad_in = mm_nt(dqkv, qkv_ref[...]).astype(BF16)
-    send_ref[...] = jnp.concatenate(sections[3] + [grad_in], 1).reshape(send_ref.shape)
-
-
-def last_kernel(recv_ref, y_first_ref, x_second_ref, grad_second_ref, out_w_ref, x_first_ref, dx_ref):
+        key_grad = mm(score_grad, split_rows(proj_ref, 0, pair))
+        value_grad = mm(weights, split_rows(flat_ref, width, pair))
+        dqkv_ref[:, at : at + lanes] = (query_grad * FACTOR).astype(BF16)
+        dqkv_ref[:, INNER + at : INNER + at + lanes] = (key_grad * FACTOR).astype(BF16)
+        dqkv_ref[:, 2 * INNER + at : 2 * INNER + at + lanes] = value_grad.astype(BF16)
+
+    for step in range(pairs + 2):
+        for stage, lag in ((score, 0), (weigh, 1), (spread, 2)):
+            if 0 <= step - lag < pairs:
+                stage(step - lag)
+    grad_in = mm_nt(dqkv_ref[...], qkv_ref[...]).astype(BF16)
+    send_ref[...] = jnp.concatenate(mixed_parts + [grad_in], 1).reshape(send_ref.shape)
+
+
+def last_kernel(
+    recv_ref, y_first_ref, normal_ref, std_ref, grad_second_ref, out_w_ref, x_first_ref, dx_ref
+):
     received = recv_ref[...].reshape(y_first_ref.shape[0], recv_ref.shape[2])
     value = mm(received[:, :INNER], out_w_ref[...])
     x_first_ref[...] = (y_first_ref[...].astype(F32) - value).astype(BF16)
     grad_in = received[:, INNER:].astype(F32)
-    dx_ref[...] = (
-        grad_second_ref[...].astype(F32) + norm_back(x_second_ref[...], grad_in)
-    ).astype(BF16)
+    grad_in = norm_back(normal_ref[...], std_ref[:, :1], grad_in)
+    dx_ref[...] = (grad_second_ref[...].astype(F32) + grad_in).astype(BF16)
 
 
 def shape_of(*sizes):
@@ -264,12 +307,17 @@
     wire = (frames, rows // frames, width + INNER)
 
     hbm = pl.BlockSpec(memory_space=pltpu.HBM)
-    sent, space_qkv, space_out = pl.pallas_call(
+    norm_shapes = (
+        jax.ShapeDtypeStruct((rows, width), F32),
+        jax.ShapeDtypeStruct((rows, 128), F32),
+    )
+    sent, space_qkv, space_out, normal_first, std_first = pl.pallas_call(
         project_kernel,
         out_shape=(
             shape_of(groups, patches, head_cols),
             shape_of(*space_qkv.shape),
             shape_of(*space_out.shape),
+            *norm_shapes,
         ),
         in_specs=[hbm] * 4,
         scratch_shapes=[
@@ -303,16 +351,22 @@
         compiler_params=PARAMS,
     )(pattern, gathered)
     returned = exchange(space_rows.reshape(groups, patches, head_cols), "space")
-    x_second, dx_first, time_send = pl.pallas_call(
+    x_second, dx_first, time_send, normal_second, std_second = pl.pallas_call(
         middle_kernel,
-        out_shape=(shape_of(rows, width), shape_of(rows, width), shape_of(*wire)),
+        out_shape=(shape_of(rows, width), shape_of(rows, width), shape_of(*wire), *norm_shapes),
         name="middle",
         compiler_params=PARAMS,
-    )(returned, y_first, y_second, grad_first, space_qkv, space_out, time_out)
+    )(returned, normal_first, std_first, y_second, grad_first, space_qkv, space_out, time_out)
     time_rows = pl.pallas_call(
         time_kernel,
         out_shape=shape_of(*wire),
-        scratch_shapes=[pltpu.VMEM((rows, width + INNER), BF16)],
+        scratch_shapes=[
+            pltpu.VMEM((rows, width + INNER), BF16),
+            pltpu.VMEM((rows, 3 * INNER), BF16),
+            pltpu.VMEM((HEADS // 2, rows, 4 * rows), F32),
+            pltpu.VMEM((HEADS // 2, rows, 4 * rows), BF16),
+            pltpu.VMEM((rows, 3 * INNER), BF16),
+        ],
         name="time_attention",
         compiler_params=PARAMS,
     )(exchange(time_send, "tm"), time_qkv)
@@ -321,7 +375,7 @@
         out_shape=(shape_of(rows, width), shape_of(rows, width)),
         name="last",
         compiler_params=PARAMS,
-    )(exchange(time_rows, "tm"), y_first, x_second, grad_second, time_out)
+    )(exchange(time_rows, "tm"), y_first, normal_second, std_second, grad_second, time_out)
     return tuple(a.reshape(shape) for a in (x_first, x_second, dx_first, dx_second))
 
 

time: 141 us -> 141 us (level)
  no operation moved by 1% of the time
where the time goes in v4:
time: 141 us; the launch traced here: 140 us
  blocking collectives  128 us (91%)
  Pallas kernels  11.7 us (8%)
    all_to_all x4, blocking collectives, exchange(): return lax.all_to_all(rows, axis, split_axis=0, concat_axis=0, tiled=True)  128 us
    pallas_call x1, Pallas kernels, per_device(): pl.pallas_call(project_kernel, out_shape=(shape_of(groups, patches, head_...  3.12 us

profile of v4, /device:TPU:1, one launch (start us, length us, event | category | flops | bytes accessed | tf_op | source)
XLA Modules:
  0.0 140.3 jit_solution(1655730025805032820)
XLA Ops:
  0.6 0.0 copy-start.6
  0.6 0.0 copy-start
  0.7 0.0 copy-start.4
  0.7 0.0 copy-start.5
  0.7 3.1 %project.1 = (bf16[16,64,256]{2,1,0:T(8,128)(2,1)S(1)}, bf16[1024,1536]{1,0:T(8,128)(2,1)S(1)}, bf16[512,1024]{1,0:T(8,128)(2,1)S(1)}, f32[128,1024]{1,0:T(8,128)S(1)}, f32[128,128]{1,0:T(8,128)S(1)}) custom-call(bf16[128,1024]{1,0:T(8,128)(2,1)} %bitcast.20, bf16[128,1024]{1,0:T(8,128)(2,1)} %bitcast.22, bf16[1024,1536]{1,0:T(8,128)(2,1)} %qkv_hbm.1, ...), custom_call_target="tpu_custom_call" | custom-call | tf_op jit(solution)/shard_map/project/pallas_call | solution.py:314
  3.8 18.8 %all_to_all.20 = bf16[16,64,256]{2,1,0:T(8,128)(2,1)S(1)} all-to-all(bf16[16,64,256]{2,1,0:T(8,128)(2,1)S(1)} %get-tuple-element.16), channel_id=1, replica_groups=mesh['tm'=64,'space'=16] {'space'}, dimensions={0} | all-to-all | bytes 1048576 | tf_op jit(solution)/shard_map/all_to_all | solution.py:291
  22.6 0.0 copy-done.6
  22.6 2.2 %space_attention.1 = bf16[1024,256]{1,0:T(8,128)(2,1)S(1)} custom-call(s32[1,8]{1,0:T(1,128)S(1)} %copy-done.6, bf16[1024,256]{1,0:T(8,128)(2,1)S(1)} %bitcast.18), custom_call_target="tpu_custom_call" | custom-call | tf_op jit(solution)/shard_map/space_attention/pallas_call | solution.py:337
  24.8 14.4 %all_to_all.21.recv_ref = bf16[16,64,256]{2,1,0:T(8,128)(2,1)S(1)} all-to-all(bf16[16,64,256]{2,1,0:T(8,128)(2,1)S(1)} %bitcast.19), channel_id=1, replica_groups=mesh['tm'=64,'space'=16] {'space'}, dimensions={0} | all-to-all | bytes 1048576 | tf_op jit(solution)/shard_map/all_to_all | solution.py:291
  39.2 0.0 copy-done
  39.2 0.0 copy-done.4
  39.2 0.0 copy-done.5
  39.2 0.0 copy-start.1
  39.2 2.7 %middle.1 = (bf16[128,1024]{1,0:T(8,128)(2,1)}, bf16[128,1024]{1,0:T(8,128)(2,1)}, bf16[64,2,1536]{2,1,0:T(2,128)(2,1)S(1)}, f32[128,1024]{1,0:T(8,128)S(1)}, f32[128,128]{1,0:T(8,128)S(1)}) custom-call(bf16[16,64,256]{2,1,0:T(8,128)(2,1)S(1)} %all_to_all.21.recv_ref, f32[128,1024]{1,0:T(8,128)S(1)} %get-tuple-element.17.normal_first_ref, ...), custom_call_target="tpu_custom_call" | custom-call | tf_op jit(solution)/shard_map/middle/pallas_call | solution.py:354
  41.9 0.0 copy-start.2
  41.9 0.0 copy-start.3
  41.9 61.5 %all_to_all.22.x_ref = bf16[64,2,1536]{2,1,0:T(2,128)(2,1)S(1)} all-to-all(bf16[64,2,1536]{2,1,0:T(2,128)(2,1)S(1)} %get-tuple-element.21), channel_id=1, replica_groups=mesh['tm'=64,'space'=16] {'tm'}, dimensions={0} | all-to-all | bytes 786432 | tf_op jit(solution)/shard_map/all_to_all | solution.py:291
  103.4 0.0 copy-done.1
  103.4 2.2 %time_attention.1 = bf16[64,2,1536]{2,1,0:T(2,128)(2,1)S(1)} custom-call(bf16[64,2,1536]{2,1,0:T(2,128)(2,1)S(1)} %all_to_all.22.x_ref, bf16[1024,1536]{1,0:T(8,128)(2,1)S(1)} %copy-done.1), custom_call_target="tpu_custom_call" | custom-call | tf_op jit(solution)/shard_map/time_attention/pallas_call | solution.py:360
  105.6 33.2 %all_to_all.23.recv_ref = bf16[64,2,1536]{2,1,0:T(2,128)(2,1)S(1)} all-to-all(bf16[64,2,1536]{2,1,0:T(2,128)(2,1)S(1)} %time_attention.1), channel_id=1, replica_groups=mesh['tm'=64,'space'=16] {'tm'}, dimensions={0} | all-to-all | bytes 786432 | tf_op jit(solution)/shard_map/all_to_all | solution.py:291
  138.8 0.0 copy-done.2
  138.8 0.0 copy-done.3
  138.8 1.5 %last.1 = (bf16[128,1024]{1,0:T(8,128)(2,1)}, bf16[128,1024]{1,0:T(8,128)(2,1)}) custom-call(bf16[64,2,1536]{2,1,0:T(2,128)(2,1)S(1)} %all_to_all.23.recv_ref, bf16[128,1024]{1,0:T(8,128)(2,1)S(1)} %bitcast.21, f32[128,1024]{1,0:T(8,128)S(1)} %get-tuple-element.22.normal_ref, f32[128,128]{1,0:T(8,128)S(1)} %get-tuple-element.23.std_ref, ...), custom_call_target="tpu_custom_call" | custom-call | tf_op jit(solution)/shard_map/last/pallas_call | solution.py:373
Async XLA Ops:
  0.6 21.9 %copy-start.6 = (s32[1,8]{1,0:T(1,128)S(1)}, s32[1,8]{1,0:T(1,128)}, u32[]{:S(2)}) copy-start(s32[1,8]{1,0:T(1,128)} %pattern_ref.1) | copy-start | bytes 100
  0.6 38.6 %copy-start = (bf16[512,1024]{1,0:T(8,128)(2,1)S(1)}, bf16[512,1024]{1,0:T(8,128)(2,1)}, u32[]{:S(2)}) copy-start(bf16[512,1024]{1,0:T(8,128)(2,1)} %out_w_ref.1) | copy-start | bytes 3145732
  0.7 38.6 %copy-start.4 = (bf16[2,1,64,1024]{3,2,1,0:T(8,128)(2,1)S(1)}, bf16[2,1,64,1024]{3,2,1,0:T(8,128)(2,1)}, u32[]{:S(2)}) copy-start(bf16[2,1,64,1024]{3,2,1,0:T(8,128)(2,1)} %param.10) | copy-start | bytes 786436
  0.7 38.6 %copy-start.5 = (bf16[2,1,64,1024]{3,2,1,0:T(8,128)(2,1)S(1)}, bf16[2,1,64,1024]{3,2,1,0:T(8,128)(2,1)}, u32[]{:S(2)}) copy-start(bf16[2,1,64,1024]{3,2,1,0:T(8,128)(2,1)} %param.11) | copy-start | bytes 786436
  39.2 64.2 %copy-start.1 = (bf16[1024,1536]{1,0:T(8,128)(2,1)S(1)}, bf16[1024,1536]{1,0:T(8,128)(2,1)}, u32[]{:S(2)}) copy-start(bf16[1024,1536]{1,0:T(8,128)(2,1)} %qkv_ref.1) | copy-start | bytes 9437188
  41.9 96.9 %copy-start.2 = (bf16[2,1,64,1024]{3,2,1,0:T(8,128)(2,1)S(1)}, bf16[2,1,64,1024]{3,2,1,0:T(8,128)(2,1)}, u32[]{:S(2)}) copy-start(bf16[2,1,64,1024]{3,2,1,0:T(8,128)(2,1)} %param.9) | copy-start | bytes 786436
  41.9 96.9 %copy-start.3 = (bf16[2,1,64,1024]{3,2,1,0:T(8,128)(2,1)S(1)}, bf16[2,1,64,1024]{3,2,1,0:T(8,128)(2,1)}, u32[]{:S(2)}) copy-start(bf16[2,1,64,1024]{3,2,1,0:T(8,128)(2,1)} %param.12) | copy-start | bytes 786436

commit v5 on v4

--- a/solution.py
+++ b/solution.py
@@ -212,7 +212,27 @@
     send_ref[...] = send_rows.reshape(send_ref.shape)
 
 
-def time_kernel(x_ref, qkv_ref, send_ref, flat_ref, proj_ref, both_ref, grads_ref, dqkv_ref):
+def time_kernel(
+    x_ref,
+    qkv_ref,
+    x_second_ref,
+    dx_first_ref,
+    send_ref,
+    x_second_hbm,
+    dx_first_hbm,
+    flat_ref,
+    proj_ref,
+    both_ref,
+    grads_ref,
+    dqkv_ref,
+    sems,
+):
+    copies = [
+        pltpu.make_async_copy(x_second_ref, x_second_hbm, sems.at[0]),
+        pltpu.make_async_copy(dx_first_ref, dx_first_hbm, sems.at[1]),
+    ]
+    for copy in copies:
+        copy.start()
     rows = x_ref.shape[0] * x_ref.shape[1]
     width = x_ref.shape[2] - INNER
     flat_ref[...] = x_ref[...].reshape(rows, width + INNER)
@@ -270,17 +290,43 @@
                 stage(step - lag)
     grad_in = mm_nt(dqkv_ref[...], qkv_ref[...]).astype(BF16)
     send_ref[...] = jnp.concatenate(mixed_parts + [grad_in], 1).reshape(send_ref.shape)
+    for copy in copies:
+        copy.wait()
 
 
 def last_kernel(
-    recv_ref, y_first_ref, normal_ref, std_ref, grad_second_ref, out_w_ref, x_first_ref, dx_ref
+    recv_ref,
+    y_first_ref,
+    normal_ref,
+    std_ref,
+    grad_second_ref,
+    out_w_ref,
+    x_first_hbm,
+    dx_hbm,
+    flat_ref,
+    x_first_ref,
+    dx_ref,
+    sems,
 ):
-    received = recv_ref[...].reshape(y_first_ref.shape[0], recv_ref.shape[2])
-    value = mm(received[:, :INNER], out_w_ref[...])
+    rows = y_first_ref.shape[0]
+    flat_ref[...] = recv_ref[...].reshape(flat_ref.shape)
+    value = mm(flat_ref[:, :INNER], out_w_ref[...])
     x_first_ref[...] = (y_first_ref[...].astype(F32) - value).astype(BF16)
-    grad_in = received[:, INNER:].astype(F32)
-    grad_in = norm_back(normal_ref[...], std_ref[:, :1], grad_in)
-    dx_ref[...] = (grad_second_ref[...].astype(F32) + grad_in).astype(BF16)
+    copies = [pltpu.make_async_copy(x_first_ref, x_first_hbm, sems.at[0])]
+    copies[0].start()
+    parts = 2
+    for i in range(parts):
+        part = slice(rows // parts * i, rows // parts * (i + 1))
+        grad_in = norm_back(
+            normal_ref[part, :], std_ref[part, :1], flat_ref[part, INNER:].astype(F32)
+        )
+        dx_ref[part, :] = (grad_second_ref[part, :].astype(F32) + grad_in).astype(BF16)
+        copies.append(
+            pltpu.make_async_copy(dx_ref.at[part, :], dx_hbm.at[part, :], sems.at[1 + i])
+        )
+        copies[-1].start()
+    for copy in copies:
+        copy.wait()
 
 
 def shape_of(*sizes):
@@ -353,26 +399,45 @@
     returned = exchange(space_rows.reshape(groups, patches, head_cols), "space")
     x_second, dx_first, time_send, normal_second, std_second = pl.pallas_call(
         middle_kernel,
-        out_shape=(shape_of(rows, width), shape_of(rows, width), shape_of(*wire), *norm_shapes),
+        out_shape=(
+            pltpu.VMEM((rows, width), BF16),
+            pltpu.VMEM((rows, width), BF16),
+            shape_of(*wire),
+            *norm_shapes,
+        ),
         name="middle",
         compiler_params=PARAMS,
     )(returned, normal_first, std_first, y_second, grad_first, space_qkv, space_out, time_out)
-    time_rows = pl.pallas_call(
+    vmem = pl.BlockSpec(memory_space=pltpu.VMEM)
+    time_rows, x_second, dx_first = pl.pallas_call(
         time_kernel,
-        out_shape=shape_of(*wire),
+        out_shape=(
+            shape_of(*wire),
+            pltpu.HBM((rows, width), BF16),
+            pltpu.HBM((rows, width), BF16),
+        ),
+        out_specs=(vmem, hbm, hbm),
         scratch_shapes=[
             pltpu.VMEM((rows, width + INNER), BF16),
             pltpu.VMEM((rows, 3 * INNER), BF16),
             pltpu.VMEM((HEADS // 2, rows, 4 * rows), F32),
             pltpu.VMEM((HEADS // 2, rows, 4 * rows), BF16),
             pltpu.VMEM((rows, 3 * INNER), BF16),
+            pltpu.SemaphoreType.DMA((2,)),
         ],
         name="time_attention",
         compiler_params=PARAMS,
-    )(exchange(time_send, "tm"), time_qkv)
+    )(exchange(time_send, "tm"), time_qkv, x_second, dx_first)
     x_first, dx_second = pl.pallas_call(
         last_kernel,
-        out_shape=(shape_of(rows, width), shape_of(rows, width)),
+        out_shape=(pltpu.HBM((rows, width), BF16), pltpu.HBM((rows, width), BF16)),
+        out_specs=(hbm, hbm),
+        scratch_shapes=[
+            pltpu.VMEM((rows, width + INNER), BF16),
+            pltpu.VMEM((rows, width), BF16),
+            pltpu.VMEM((rows, width), BF16),
+            pltpu.SemaphoreType.DMA((3,)),
+        ],
         name="last",
         compiler_params=PARAMS,
     )(exchange(time_rows, "tm"), y_first, normal_second, std_second, grad_second, time_out)

time: 141 us -> 140 us (level)
  no operation moved by 1% of the time
where the time goes in v5:
time: 140 us
  blocking collectives  128 us (91%)
  Pallas kernels  10.9 us (8%)
    all_to_all x4, blocking collectives, exchange(): return lax.all_to_all(rows, axis, split_axis=0, concat_axis=0, tiled=True)  128 us
    pallas_call x1, Pallas kernels, per_device(): pl.pallas_call(project_kernel, out_shape=(shape_of(groups, patches, head_...  3.12 us

profile of v5, /device:TPU:1, one launch (start us, length us, event | category | flops | bytes accessed | tf_op | source)
XLA Modules:
  0.0 139.5 jit_solution(18247329504153304916)
XLA Ops:
  0.6 0.0 copy-start.6
  0.6 0.0 copy-start
  0.7 0.0 copy-start.4
  0.7 0.0 copy-start.5
  0.7 3.1 %project.1 = (bf16[16,64,256]{2,1,0:T(8,128)(2,1)S(1)}, bf16[1024,1536]{1,0:T(8,128)(2,1)S(1)}, bf16[512,1024]{1,0:T(8,128)(2,1)S(1)}, f32[128,1024]{1,0:T(8,128)S(1)}, f32[128,128]{1,0:T(8,128)S(1)}) custom-call(bf16[128,1024]{1,0:T(8,128)(2,1)} %bitcast.20, bf16[128,1024]{1,0:T(8,128)(2,1)} %bitcast.22, bf16[1024,1536]{1,0:T(8,128)(2,1)} %qkv_hbm.1, ...), custom_call_target="tpu_custom_call" | custom-call | tf_op jit(solution)/shard_map/project/pallas_call | solution.py:360
  3.8 18.8 %all_to_all.20 = bf16[16,64,256]{2,1,0:T(8,128)(2,1)S(1)} all-to-all(bf16[16,64,256]{2,1,0:T(8,128)(2,1)S(1)} %get-tuple-element.19), channel_id=1, replica_groups=mesh['tm'=64,'space'=16] {'space'}, dimensions={0} | all-to-all | bytes 1048576 | tf_op jit(solution)/shard_map/all_to_all | solution.py:337
  22.6 0.0 copy-done.6
  22.6 2.2 %space_attention.1 = bf16[1024,256]{1,0:T(8,128)(2,1)S(1)} custom-call(s32[1,8]{1,0:T(1,128)S(1)} %copy-done.6, bf16[1024,256]{1,0:T(8,128)(2,1)S(1)} %bitcast.18), custom_call_target="tpu_custom_call" | custom-call | tf_op jit(solution)/shard_map/space_attention/pallas_call | solution.py:383
  24.8 14.4 %all_to_all.21.recv_ref = bf16[16,64,256]{2,1,0:T(8,128)(2,1)S(1)} all-to-all(bf16[16,64,256]{2,1,0:T(8,128)(2,1)S(1)} %bitcast.19), channel_id=1, replica_groups=mesh['tm'=64,'space'=16] {'space'}, dimensions={0} | all-to-all | bytes 1048576 | tf_op jit(solution)/shard_map/all_to_all | solution.py:337
  39.2 0.0 copy-done
  39.2 0.0 copy-done.4
  39.2 0.0 copy-done.5
  39.2 0.0 copy-start.1
  39.3 2.0 %middle.1 = (bf16[128,1024]{1,0:T(8,128)(2,1)S(1)}, bf16[128,1024]{1,0:T(8,128)(2,1)S(1)}, bf16[64,2,1536]{2,1,0:T(2,128)(2,1)S(1)}, f32[128,1024]{1,0:T(8,128)S(1)}, f32[128,128]{1,0:T(8,128)S(1)}) custom-call(bf16[16,64,256]{2,1,0:T(8,128)(2,1)S(1)} %all_to_all.21.recv_ref, f32[128,1024]{1,0:T(8,128)S(1)} %get-tuple-element.20.normal_first_ref, ...), custom_call_target="tpu_custom_call" | custom-call | tf_op jit(solution)/shard_map/middle/pallas_call | solution.py:400
  41.3 0.0 copy-start.2
  41.3 0.0 copy-start.3
  41.3 61.5 %all_to_all.22.x_ref = bf16[64,2,1536]{2,1,0:T(2,128)(2,1)S(1)} all-to-all(bf16[64,2,1536]{2,1,0:T(2,128)(2,1)S(1)} %get-tuple-element.24), channel_id=1, replica_groups=mesh['tm'=64,'space'=16] {'tm'}, dimensions={0} | all-to-all | bytes 786432 | tf_op jit(solution)/shard_map/all_to_all | solution.py:337
  102.8 0.0 copy-done.1
  102.8 2.2 %time_attention.1 = (bf16[64,2,1536]{2,1,0:T(2,128)(2,1)S(1)}, bf16[128,1024]{1,0:T(8,128)(2,1)}, bf16[128,1024]{1,0:T(8,128)(2,1)}) custom-call(bf16[64,2,1536]{2,1,0:T(2,128)(2,1)S(1)} %all_to_all.22.x_ref, bf16[1024,1536]{1,0:T(8,128)(2,1)S(1)} %copy-done.1, bf16[128,1024]{1,0:T(8,128)(2,1)S(1)} %get-tuple-element.25.x_second_ref, ...), custom_call_target="tpu_custom_call" | custom-call | tf_op jit(solution)/shard_map/time_attention/pallas_call | solution.py:412
  105.0 33.2 %all_to_all.23.recv_ref = bf16[64,2,1536]{2,1,0:T(2,128)(2,1)S(1)} all-to-all(bf16[64,2,1536]{2,1,0:T(2,128)(2,1)S(1)} %get-tuple-element.27), channel_id=1, replica_groups=mesh['tm'=64,'space'=16] {'tm'}, dimensions={0} | all-to-all | bytes 786432 | tf_op jit(solution)/shard_map/all_to_all | solution.py:337
  138.2 0.0 copy-done.2
  138.2 0.0 copy-done.3
  138.2 1.3 last.1
Async XLA Ops:
  0.6 22.0 %copy-start.6 = (s32[1,8]{1,0:T(1,128)S(1)}, s32[1,8]{1,0:T(1,128)}, u32[]{:S(2)}) copy-start(s32[1,8]{1,0:T(1,128)} %pattern_ref.1) | copy-start | bytes 100
  0.6 38.6 %copy-start = (bf16[512,1024]{1,0:T(8,128)(2,1)S(1)}, bf16[512,1024]{1,0:T(8,128)(2,1)}, u32[]{:S(2)}) copy-start(bf16[512,1024]{1,0:T(8,128)(2,1)} %out_w_ref.1) | copy-start | bytes 3145732
  0.7 38.6 %copy-start.4 = (bf16[2,1,64,1024]{3,2,1,0:T(8,128)(2,1)S(1)}, bf16[2,1,64,1024]{3,2,1,0:T(8,128)(2,1)}, u32[]{:S(2)}) copy-start(bf16[2,1,64,1024]{3,2,1,0:T(8,128)(2,1)} %param.10) | copy-start | bytes 786436
  0.7 38.6 %copy-start.5 = (bf16[2,1,64,1024]{3,2,1,0:T(8,128)(2,1)S(1)}, bf16[2,1,64,1024]{3,2,1,0:T(8,128)(2,1)}, u32[]{:S(2)}) copy-start(bf16[2,1,64,1024]{3,2,1,0:T(8,128)(2,1)} %param.11) | copy-start | bytes 786436
  39.2 63.6 %copy-start.1 = (bf16[1024,1536]{1,0:T(8,128)(2,1)S(1)}, bf16[1024,1536]{1,0:T(8,128)(2,1)}, u32[]{:S(2)}) copy-start(bf16[1024,1536]{1,0:T(8,128)(2,1)} %qkv_ref.1) | copy-start | bytes 9437188
  41.3 97.0 %copy-start.2 = (bf16[2,1,64,1024]{3,2,1,0:T(8,128)(2,1)S(1)}, bf16[2,1,64,1024]{3,2,1,0:T(8,128)(2,1)}, u32[]{:S(2)}) copy-start(bf16[2,1,64,1024]{3,2,1,0:T(8,128)(2,1)} %param.9) | copy-start | bytes 786436
  41.3 96.9 %copy-start.3 = (bf16[2,1,64,1024]{3,2,1,0:T(8,128)(2,1)S(1)}, bf16[2,1,64,1024]{3,2,1,0:T(8,128)(2,1)}, u32[]{:S(2)}) copy-start(bf16[2,1,64,1024]{3,2,1,0:T(8,128)(2,1)} %param.12) | copy-start | bytes 786436

commit v6 on v5

--- a/solution.py
+++ b/solution.py
@@ -120,7 +120,29 @@
     assemble(keys, projected(2), 1)
 
 
-def space_kernel(pattern_ref, x_ref, out_ref, both_ref, grads_ref, own_ref, beside_ref):
+def space_kernel(
+    pattern_ref,
+    x_ref,
+    y_second_hbm,
+    grad_first_hbm,
+    time_out_hbm,
+    out_ref,
+    y_second_ref,
+    grad_first_ref,
+    time_out_ref,
+    both_ref,
+    grads_ref,
+    own_ref,
+    beside_ref,
+    sems,
+):
+    copies = [
+        pltpu.make_async_copy(y_second_hbm, y_second_ref, sems.at[0]),
+        pltpu.make_async_copy(grad_first_hbm, grad_first_ref, sems.at[1]),
+        pltpu.make_async_copy(time_out_hbm, time_out_ref, sems.at[2]),
+    ]
+    for copy in copies:
+        copy.start()
     width = 2 * HEAD_DIM
     blocks = pattern_ref.shape[1]
     block = x_ref.shape[0] // blocks
@@ -154,8 +176,8 @@
         own_ref[rows_of(b), :] = key_out[:block]
         beside_ref[rows_of(b), :] = key_out[block:]
 
-    for step in range(blocks + 2):
-        for stage, lag in ((score, 0), (weigh, 1), (spread, 2)):
+    for step in range(blocks + 3):
+        for stage, lag in ((score, 0), (weigh, 2), (spread, 3)):
             if 0 <= step - lag < blocks:
                 stage(step - lag)
     for b in range(blocks):
@@ -164,6 +186,8 @@
             part = beside_ref[rows_of(other), :]
             total = total + jnp.where(pattern_ref[0, other] == b, part, 0.0)
         out_ref[rows_of(b), width:] = (total * scale).astype(BF16)
+    for copy in copies:
+        copy.wait()
 
 
 def middle_kernel(
@@ -353,6 +377,7 @@
     wire = (frames, rows // frames, width + INNER)
 
     hbm = pl.BlockSpec(memory_space=pltpu.HBM)
+    vmem = pl.BlockSpec(memory_space=pltpu.VMEM)
     norm_shapes = (
         jax.ShapeDtypeStruct((rows, width), F32),
         jax.ShapeDtypeStruct((rows, 128), F32),
@@ -380,22 +405,32 @@
         ]
     )
     gathered = exchange(sent, "space").reshape(groups * patches, head_cols)
-    space_rows = pl.pallas_call(
+    space_rows, y_second, grad_first, time_out = pl.pallas_call(
         space_kernel,
-        out_shape=shape_of(groups * patches, head_cols),
-        in_specs=[
-            pl.BlockSpec(memory_space=pltpu.SMEM),
-            pl.BlockSpec(memory_space=pltpu.VMEM),
-        ],
+        out_shape=(
+            shape_of(groups * patches, head_cols),
+            pltpu.VMEM((rows, width), BF16),
+            pltpu.VMEM((rows, width), BF16),
+            pltpu.VMEM(time_out.shape, BF16),
+        ),
+        in_specs=[pl.BlockSpec(memory_space=pltpu.SMEM), vmem, hbm, hbm, hbm],
         scratch_shapes=[
             pltpu.VMEM((blocks, 2 * block, 2 * block), F32),
             pltpu.VMEM((blocks, 2 * block, 2 * block), BF16),
             pltpu.VMEM((groups * patches, 2 * HEAD_DIM), F32),
             pltpu.VMEM((groups * patches, 2 * HEAD_DIM), F32),
+            pltpu.SemaphoreType.DMA((3,)),
         ],
         name="space_attention",
         compiler_params=PARAMS,
-    )(pattern, gathered)
+    )(
+        pattern,
+        gathered,
+        *[
+            pltpu.with_memory_space_constraint(a, pltpu.HBM)
+            for a in (y_second, grad_first, time_out)
+        ],
+    )
     returned = exchange(space_rows.reshape(groups, patches, head_cols), "space")
     x_second, dx_first, time_send, normal_second, std_second = pl.pallas_call(
         middle_kernel,
@@ -408,7 +443,6 @@
         name="middle",
         compiler_params=PARAMS,
     )(returned, normal_first, std_first, y_second, grad_first, space_qkv, space_out, time_out)
-    vmem = pl.BlockSpec(memory_space=pltpu.VMEM)
     time_rows, x_second, dx_first = pl.pallas_call(
         time_kernel,
         out_shape=(

time: 140 us -> 141 us (level)
  no operation moved by 1% of the time
where the time goes in v6:
time: 141 us; the launch traced here: 140 us
  blocking collectives  128 us (91%)
  Pallas kernels  11.8 us (8%)
    all_to_all x4, blocking collectives, exchange(): return lax.all_to_all(rows, axis, split_axis=0, concat_axis=0, tiled=True)  128 us
    pallas_call x1, Pallas kernels, per_device(): pl.pallas_call(space_kernel, out_shape=(shape_of(groups * patches, head_c...  3.35 us
    pallas_call x1, Pallas kernels, per_device(): pl.pallas_call(project_kernel, out_shape=(shape_of(groups, patches, head_...  3.02 us

profile of v6, /device:TPU:1, one launch (start us, length us, event | category | flops | bytes accessed | tf_op | source)
XLA Modules:
  0.0 140.4 jit_solution(2703350096448049611)
XLA Ops:
  0.6 0.0 copy-start.3
  0.6 3.0 %project.1 = (bf16[16,64,256]{2,1,0:T(8,128)(2,1)S(1)}, bf16[1024,1536]{1,0:T(8,128)(2,1)S(1)}, bf16[512,1024]{1,0:T(8,128)(2,1)S(1)}, f32[128,1024]{1,0:T(8,128)S(1)}, f32[128,128]{1,0:T(8,128)S(1)}) custom-call(bf16[128,1024]{1,0:T(8,128)(2,1)} %bitcast.19, bf16[128,1024]{1,0:T(8,128)(2,1)} %bitcast.21, bf16[1024,1536]{1,0:T(8,128)(2,1)} %qkv_hbm.1, ...), custom_call_target="tpu_custom_call" | custom-call | tf_op jit(solution)/shard_map/project/pallas_call | solution.py:385
  3.7 18.8 %all_to_all.20 = bf16[16,64,256]{2,1,0:T(8,128)(2,1)S(1)} all-to-all(bf16[16,64,256]{2,1,0:T(8,128)(2,1)S(1)} %get-tuple-element.23), channel_id=1, replica_groups=mesh['tm'=64,'space'=16] {'space'}, dimensions={0} | all-to-all | bytes 1048576 | tf_op jit(solution)/shard_map/all_to_all | solution.py:361
  22.4 0.0 copy-done.3
  22.4 3.4 %space_attention.1 = (bf16[1024,256]{1,0:T(8,128)(2,1)S(1)}, bf16[128,1024]{1,0:T(8,128)(2,1)S(1)}, bf16[128,1024]{1,0:T(8,128)(2,1)S(1)}, bf16[512,1024]{1,0:T(8,128)(2,1)S(1)}) custom-call(s32[1,8]{1,0:T(1,128)S(1)} %copy-done.3, bf16[1024,256]{1,0:T(8,128)(2,1)S(1)} %bitcast.18, bf16[128,1024]{1,0:T(8,128)(2,1)} %bitcast.24, bf16[128,1024]{1,0:T(8,128)(2,1)} %bitcast.25, ...), custom_call_target="tpu_custom_call" | custom-call | tf_op jit(solution)/shard_map/space_attention/pallas_call | solution.py:408
  25.8 14.4 %all_to_all.21.recv_ref = bf16[16,64,256]{2,1,0:T(8,128)(2,1)S(1)} all-to-all(bf16[16,64,256]{2,1,0:T(8,128)(2,1)S(1)} %bitcast.23), channel_id=1, replica_groups=mesh['tm'=64,'space'=16] {'space'}, dimensions={0} | all-to-all | bytes 1048576 | tf_op jit(solution)/shard_map/all_to_all | solution.py:361
  40.2 0.0 copy-start
  40.2 2.0 %middle.1 = (bf16[128,1024]{1,0:T(8,128)(2,1)S(1)}, bf16[128,1024]{1,0:T(8,128)(2,1)S(1)}, bf16[64,2,1536]{2,1,0:T(2,128)(2,1)S(1)}, f32[128,1024]{1,0:T(8,128)S(1)}, f32[128,128]{1,0:T(8,128)S(1)}) custom-call(bf16[16,64,256]{2,1,0:T(8,128)(2,1)S(1)} %all_to_all.21.recv_ref, f32[128,1024]{1,0:T(8,128)S(1)} %get-tuple-element.25.normal_first_ref, ...), custom_call_target="tpu_custom_call" | custom-call | tf_op jit(solution)/shard_map/middle/pallas_call | solution.py:435
  42.2 0.0 copy-start.1
  42.2 0.0 copy-start.2
  42.2 61.5 %all_to_all.22.x_ref = bf16[64,2,1536]{2,1,0:T(2,128)(2,1)S(1)} all-to-all(bf16[64,2,1536]{2,1,0:T(2,128)(2,1)S(1)} %get-tuple-element.32), channel_id=1, replica_groups=mesh['tm'=64,'space'=16] {'tm'}, dimensions={0} | all-to-all | bytes 786432 | tf_op jit(solution)/shard_map/all_to_all | solution.py:361
  103.7 0.0 copy-done
  103.7 2.2 %time_attention.1 = (bf16[64,2,1536]{2,1,0:T(2,128)(2,1)S(1)}, bf16[128,1024]{1,0:T(8,128)(2,1)}, bf16[128,1024]{1,0:T(8,128)(2,1)}) custom-call(bf16[64,2,1536]{2,1,0:T(2,128)(2,1)S(1)} %all_to_all.22.x_ref, bf16[1024,1536]{1,0:T(8,128)(2,1)S(1)} %copy-done, bf16[128,1024]{1,0:T(8,128)(2,1)S(1)} %get-tuple-element.33.x_second_ref, ...), custom_call_target="tpu_custom_call" | custom-call | tf_op jit(solution)/shard_map/time_attention/pallas_call | solution.py:446
  106.0 33.2 %all_to_all.23.recv_ref = bf16[64,2,1536]{2,1,0:T(2,128)(2,1)S(1)} all-to-all(bf16[64,2,1536]{2,1,0:T(2,128)(2,1)S(1)} %get-tuple-element.35), channel_id=1, replica_groups=mesh['tm'=64,'space'=16] {'tm'}, dimensions={0} | all-to-all | bytes 786432 | tf_op jit(solution)/shard_map/all_to_all | solution.py:361
  139.1 0.0 copy-done.1
  139.1 0.0 copy-done.2
  139.1 1.3 last.1
Async XLA Ops:
  0.6 21.8 %copy-start.3 = (s32[1,8]{1,0:T(1,128)S(1)}, s32[1,8]{1,0:T(1,128)}, u32[]{:S(2)}) copy-start(s32[1,8]{1,0:T(1,128)} %pattern_ref.1) | copy-start | bytes 100
  40.2 63.5 %copy-start = (bf16[1024,1536]{1,0:T(8,128)(2,1)S(1)}, bf16[1024,1536]{1,0:T(8,128)(2,1)}, u32[]{:S(2)}) copy-start(bf16[1024,1536]{1,0:T(8,128)(2,1)} %qkv_ref.1) | copy-start | bytes 9437188
  42.2 96.9 %copy-start.1 = (bf16[2,1,64,1024]{3,2,1,0:T(8,128)(2,1)S(1)}, bf16[2,1,64,1024]{3,2,1,0:T(8,128)(2,1)}, u32[]{:S(2)}) copy-start(bf16[2,1,64,1024]{3,2,1,0:T(8,128)(2,1)} %param.9) | copy-start | bytes 786436
  42.2 96.9 %copy-start.2 = (bf16[2,1,64,1024]{3,2,1,0:T(8,128)(2,1)S(1)}, bf16[2,1,64,1024]{3,2,1,0:T(8,128)(2,1)}, u32[]{:S(2)}) copy-start(bf16[2,1,64,1024]{3,2,1,0:T(8,128)(2,1)} %param.12) | copy-start | bytes 786436

commit v7 on v5

--- a/solution.py
+++ b/solution.py
@@ -154,8 +154,8 @@
         own_ref[rows_of(b), :] = key_out[:block]
         beside_ref[rows_of(b), :] = key_out[block:]
 
-    for step in range(blocks + 2):
-        for stage, lag in ((score, 0), (weigh, 1), (spread, 2)):
+    for step in range(blocks + 3):
+        for stage, lag in ((score, 0), (weigh, 2), (spread, 3)):
             if 0 <= step - lag < blocks:
                 stage(step - lag)
     for b in range(blocks):
@@ -314,7 +314,7 @@
     x_first_ref[...] = (y_first_ref[...].astype(F32) - value).astype(BF16)
     copies = [pltpu.make_async_copy(x_first_ref, x_first_hbm, sems.at[0])]
     copies[0].start()
-    parts = 2
+    parts = 4
     for i in range(parts):
         part = slice(rows // parts * i, rows // parts * (i + 1))
         grad_in = norm_back(
@@ -436,7 +436,7 @@
             pltpu.VMEM((rows, width + INNER), BF16),
             pltpu.VMEM((rows, width), BF16),
             pltpu.VMEM((rows, width), BF16),
-            pltpu.SemaphoreType.DMA((3,)),
+            pltpu.SemaphoreType.DMA((5,)),
         ],
         name="last",
         compiler_params=PARAMS,

time: 140 us -> 140 us (level)
  no operation moved by 1% of the time
where the time goes in v7:
time: 140 us; the launch traced here: 139 us
  blocking collectives  128 us (91%)
  Pallas kernels  10.8 us (8%)
    all_to_all x4, blocking collectives, exchange(): return lax.all_to_all(rows, axis, split_axis=0, concat_axis=0, tiled=True)  128 us
    pallas_call x1, Pallas kernels, per_device(): pl.pallas_call(project_kernel, out_shape=(shape_of(groups, patches, head_...  3.12 us

profile of v7, /device:TPU:1, one launch (start us, length us, event | category | flops | bytes accessed | tf_op | source)
XLA Modules:
  0.0 139.4 jit_solution(16713056162085254043)
XLA Ops:
  0.6 0.0 copy-start.6
  0.6 0.0 copy-start
  0.7 0.0 copy-start.4
  0.7 0.0 copy-start.5
  0.7 3.1 %project.1 = (bf16[16,64,256]{2,1,0:T(8,128)(2,1)S(1)}, bf16[1024,1536]{1,0:T(8,128)(2,1)S(1)}, bf16[512,1024]{1,0:T(8,128)(2,1)S(1)}, f32[128,1024]{1,0:T(8,128)S(1)}, f32[128,128]{1,0:T(8,128)S(1)}) custom-call(bf16[128,1024]{1,0:T(8,128)(2,1)} %bitcast.20, bf16[128,1024]{1,0:T(8,128)(2,1)} %bitcast.22, bf16[1024,1536]{1,0:T(8,128)(2,1)} %qkv_hbm.1, ...), custom_call_target="tpu_custom_call" | custom-call | tf_op jit(solution)/shard_map/project/pallas_call | solution.py:360
  3.8 18.8 %all_to_all.20 = bf16[16,64,256]{2,1,0:T(8,128)(2,1)S(1)} all-to-all(bf16[16,64,256]{2,1,0:T(8,128)(2,1)S(1)} %get-tuple-element.19), channel_id=1, replica_groups=mesh['tm'=64,'space'=16] {'space'}, dimensions={0} | all-to-all | bytes 1048576 | tf_op jit(solution)/shard_map/all_to_all | solution.py:337
  22.6 0.0 copy-done.6
  22.6 2.1 %space_attention.1 = bf16[1024,256]{1,0:T(8,128)(2,1)S(1)} custom-call(s32[1,8]{1,0:T(1,128)S(1)} %copy-done.6, bf16[1024,256]{1,0:T(8,128)(2,1)S(1)} %bitcast.18), custom_call_target="tpu_custom_call" | custom-call | tf_op jit(solution)/shard_map/space_attention/pallas_call | solution.py:383
  24.7 14.4 %all_to_all.21.recv_ref = bf16[16,64,256]{2,1,0:T(8,128)(2,1)S(1)} all-to-all(bf16[16,64,256]{2,1,0:T(8,128)(2,1)S(1)} %bitcast.19), channel_id=1, replica_groups=mesh['tm'=64,'space'=16] {'space'}, dimensions={0} | all-to-all | bytes 1048576 | tf_op jit(solution)/shard_map/all_to_all | solution.py:337
  39.1 0.0 copy-done
  39.1 0.0 copy-done.4
  39.1 0.0 copy-done.5
  39.1 0.0 copy-start.1
  39.2 2.0 %middle.1 = (bf16[128,1024]{1,0:T(8,128)(2,1)S(1)}, bf16[128,1024]{1,0:T(8,128)(2,1)S(1)}, bf16[64,2,1536]{2,1,0:T(2,128)(2,1)S(1)}, f32[128,1024]{1,0:T(8,128)S(1)}, f32[128,128]{1,0:T(8,128)S(1)}) custom-call(bf16[16,64,256]{2,1,0:T(8,128)(2,1)S(1)} %all_to_all.21.recv_ref, f32[128,1024]{1,0:T(8,128)S(1)} %get-tuple-element.20.normal_first_ref, ...), custom_call_target="tpu_custom_call" | custom-call | tf_op jit(solution)/shard_map/middle/pallas_call | solution.py:400
  41.2 0.0 copy-start.2
  41.2 0.0 copy-start.3
  41.2 61.5 %all_to_all.22.x_ref = bf16[64,2,1536]{2,1,0:T(2,128)(2,1)S(1)} all-to-all(bf16[64,2,1536]{2,1,0:T(2,128)(2,1)S(1)} %get-tuple-element.24), channel_id=1, replica_groups=mesh['tm'=64,'space'=16] {'tm'}, dimensions={0} | all-to-all | bytes 786432 | tf_op jit(solution)/shard_map/all_to_all | solution.py:337
  102.7 0.0 copy-done.1
  102.7 2.2 %time_attention.1 = (bf16[64,2,1536]{2,1,0:T(2,128)(2,1)S(1)}, bf16[128,1024]{1,0:T(8,128)(2,1)}, bf16[128,1024]{1,0:T(8,128)(2,1)}) custom-call(bf16[64,2,1536]{2,1,0:T(2,128)(2,1)S(1)} %all_to_all.22.x_ref, bf16[1024,1536]{1,0:T(8,128)(2,1)S(1)} %copy-done.1, bf16[128,1024]{1,0:T(8,128)(2,1)S(1)} %get-tuple-element.25.x_second_ref, ...), custom_call_target="tpu_custom_call" | custom-call | tf_op jit(solution)/shard_map/time_attention/pallas_call | solution.py:412
  104.9 33.2 %all_to_all.23.recv_ref = bf16[64,2,1536]{2,1,0:T(2,128)(2,1)S(1)} all-to-all(bf16[64,2,1536]{2,1,0:T(2,128)(2,1)S(1)} %get-tuple-element.27), channel_id=1, replica_groups=mesh['tm'=64,'space'=16] {'tm'}, dimensions={0} | all-to-all | bytes 786432 | tf_op jit(solution)/shard_map/all_to_all | solution.py:337
  138.1 0.0 copy-done.2
  138.1 0.0 copy-done.3
  138.1 1.3 last.1
Async XLA Ops:
  0.6 22.0 %copy-start.6 = (s32[1,8]{1,0:T(1,128)S(1)}, s32[1,8]{1,0:T(1,128)}, u32[]{:S(2)}) copy-start(s32[1,8]{1,0:T(1,128)} %pattern_ref.1) | copy-start | bytes 100
  0.6 38.5 %copy-start = (bf16[512,1024]{1,0:T(8,128)(2,1)S(1)}, bf16[512,1024]{1,0:T(8,128)(2,1)}, u32[]{:S(2)}) copy-start(bf16[512,1024]{1,0:T(8,128)(2,1)} %out_w_ref.1) | copy-start | bytes 3145732
  0.7 38.5 %copy-start.4 = (bf16[2,1,64,1024]{3,2,1,0:T(8,128)(2,1)S(1)}, bf16[2,1,64,1024]{3,2,1,0:T(8,128)(2,1)}, u32[]{:S(2)}) copy-start(bf16[2,1,64,1024]{3,2,1,0:T(8,128)(2,1)} %param.10) | copy-start | bytes 786436
  0.7 38.5 %copy-start.5 = (bf16[2,1,64,1024]{3,2,1,0:T(8,128)(2,1)S(1)}, bf16[2,1,64,1024]{3,2,1,0:T(8,128)(2,1)}, u32[]{:S(2)}) copy-start(bf16[2,1,64,1024]{3,2,1,0:T(8,128)(2,1)} %param.11) | copy-start | bytes 786436
  39.1 63.6 %copy-start.1 = (bf16[1024,1536]{1,0:T(8,128)(2,1)S(1)}, bf16[1024,1536]{1,0:T(8,128)(2,1)}, u32[]{:S(2)}) copy-start(bf16[1024,1536]{1,0:T(8,128)(2,1)} %qkv_ref.1) | copy-start | bytes 9437188
  41.2 96.9 %copy-start.2 = (bf16[2,1,64,1024]{3,2,1,0:T(8,128)(2,1)S(1)}, bf16[2,1,64,1024]{3,2,1,0:T(8,128)(2,1)}, u32[]{:S(2)}) copy-start(bf16[2,1,64,1024]{3,2,1,0:T(8,128)(2,1)} %param.9) | copy-start | bytes 786436
  41.2 96.9 %copy-start.3 = (bf16[2,1,64,1024]{3,2,1,0:T(8,128)(2,1)S(1)}, bf16[2,1,64,1024]{3,2,1,0:T(8,128)(2,1)}, u32[]{:S(2)}) copy-start(bf16[2,1,64,1024]{3,2,1,0:T(8,128)(2,1)} %param.12) | copy-start | bytes 786436
